TPU v7x, 32 devices: a whole 2x2x4 slice. The times are simulated.
32 devices in a mesh: dp: 16 (over z, y, x), tensor: 2 (over core).
Axes of the slice: x: 2, y: 2, z: 4, core: 2. Of those that a mesh axis runs over, the one named last changes fastest.
Arguments:
- inputs: bfloat16 [25088, 512], P(('dp', 'tensor')), may hold values from -6 to 6
- cotangent: bfloat16 [25088, 512], P(('dp', 'tensor')), may hold values from -6 to 6
- region_ids: int32 [196], replicated, may hold values from 0 to 3
- rel_index: int32 [49, 49], replicated, may hold values from 0 to 168
- norm1_gain: bfloat16 [2, 512], replicated, may hold values from 0.5 to 1.5
- norm1_bias: bfloat16 [2, 512], replicated, may hold values from -1.75 to 1.75
- w_qkv: bfloat16 [2, 3, 512, 512], P(None, None, 'dp', 'tensor'), may hold values from -0.25 to 0.25
- qv_bias: bfloat16 [2, 2, 512], P(None, None, 'tensor'), may hold values from -1.75 to 1.75
- bias_table: bfloat16 [2, 16, 169], P(None, 'tensor'), may hold values from -3 to 250
- w_proj: bfloat16 [2, 512, 512], P(None, 'tensor', 'dp'), may hold values from -0.75 to 0.75
- proj_bias: bfloat16 [2, 512], replicated, may hold values from -1.75 to 1.75
- norm2_gain: bfloat16 [2, 512], replicated, may hold values from 0.5 to 1.5
- norm2_bias: bfloat16 [2, 512], replicated, may hold values from -1.75 to 1.75
- w_fc1: bfloat16 [2, 512, 2048], P(None, 'dp', 'tensor'), may hold values from -0.25 to 0.25
- fc1_bias: bfloat16 [2, 2048], P(None, 'tensor'), may hold values from -3 to 3
- w_fc2: bfloat16 [2, 2048, 512], P(None, 'tensor', 'dp'), may hold values from -0.125 to 0.125
- fc2_bias: bfloat16 [2, 512], replicated, may hold values from -1.75 to 1.75
Outputs:
- outputs: float32 [25088, 512], P(('dp', 'tensor'))
- input_grad: float32 [25088, 512], P(('dp', 'tensor'))
- norm1_gain_grad: float32 [2, 512], replicated
- norm1_bias_grad: float32 [2, 512], replicated
- w_qkv_grad: float32 [2, 3, 512, 512], P(None, None, 'dp', 'tensor')
- qv_bias_grad: float32 [2, 2, 512], P(None, None, 'tensor')
- bias_table_grad: float32 [2, 16, 169], P(None, 'tensor')
- w_proj_grad: float32 [2, 512, 512], P(None, 'tensor', 'dp')
- proj_bias_grad: float32 [2, 512], replicated
- norm2_gain_grad: float32 [2, 512], replicated
- norm2_bias_grad: float32 [2, 512], replicated
- w_fc1_grad: float32 [2, 512, 2048], P(None, 'dp', 'tensor')
- fc1_bias_grad: float32 [2, 2048], P(None, 'tensor')
- w_fc2_grad: float32 [2, 2048, 512], P(None, 'tensor', 'dp')
- fc2_bias_grad: float32 [2, 512], replicated
All inputs are finite; a program needn't handle non-finite values.
Results may differ from a plain program's by a relative error of at most 0.025.
Values may be sent and summed in bfloat16 or wider, within the bound.
A program may use at most 192 MiB of HBM per device.

v0:
```python
import jax
import jax.numpy as jnp
from jax import lax
from jax.sharding import PartitionSpec as P

HD = 32
GRID = 14
WIN = 7
SHIFT = 3
LAYERS = 2
TABLE = 169


EPS = 1e-05
MASKED = -100.0
EXACT_PRECISION = lax.Precision.HIGHEST


def to_grid(tokens, images):
    per_side = GRID // WIN
    shaped = tokens.reshape(images, per_side, per_side, WIN, WIN, -1)
    return shaped.transpose(0, 1, 3, 2, 4, 5).reshape(images, GRID, GRID, -1)


def to_windows(grid_rows, images):
    per_side = GRID // WIN
    shaped = grid_rows.reshape(images, per_side, WIN, per_side, WIN, -1)
    return shaped.transpose(0, 1, 3, 2, 4, 5).reshape(images * GRID * GRID, -1)


def rolled(tokens, images, offset):
    return to_windows(jnp.roll(to_grid(tokens, images), offset, axis=(1, 2)), images)


def normalize(residual):
    average = jnp.mean(residual, -1, keepdims=True)
    centered = residual - average
    inverse = lax.rsqrt(jnp.mean(centered * centered, -1, keepdims=True) + EPS)
    return (centered * inverse, inverse)


def norm_back(grad_out, normed, inverse, gain_value):
    scaled = grad_out * gain_value
    return inverse * (
        scaled
        - jnp.mean(scaled, -1, keepdims=True)
        - normed * jnp.mean(scaled * normed, -1, keepdims=True)
    )


def gelu_parts(hidden_pre):
    cumulative = 0.5 * (1.0 + lax.erf(hidden_pre * 0.7071067811865476))
    density = jnp.exp(-0.5 * hidden_pre * hidden_pre) * 0.3989422804014327
    return (hidden_pre * cumulative, cumulative + hidden_pre * density)


def product(first_operand, second_operand):
    return jnp.dot(first_operand, second_operand, preferred_element_type=jnp.float32)


def mixed_einsum(pattern, first_operand, second_operand):
    return jnp.einsum(pattern, first_operand, second_operand, preferred_element_type=jnp.float32)


def exact_einsum(pattern, first_operand, second_operand):
    return jnp.einsum(pattern, first_operand, second_operand, precision=EXACT_PRECISION)


def per_device(
    inputs,
    cotangent,
    region_ids,
    rel_index,
    norm1_gain,
    norm1_bias,
    w_qkv,
    qv_bias,
    bias_table,
    w_proj,
    proj_bias,
    norm2_gain,
    norm2_bias,
    w_fc1,
    fc1_bias,
    w_fc2,
    fc2_bias,
):
    groups = lax.axis_size("tensor")
    gathered_rows = inputs.shape[0] * groups
    images = gathered_rows // (GRID * GRID)
    heads_local = bias_table.shape[1]
    width_local = heads_local * HD
    per_side = GRID // WIN
    windows = per_side * per_side
    win_tokens = WIN * WIN
    score_scale = HD ** (-0.5)
    head_shape = (images, windows, win_tokens, heads_local, HD)
    one_hot = (rel_index[:, :, None] == jnp.arange(TABLE, dtype=jnp.int32)[None, None, :]).astype(
        jnp.float32
    )
    regions = region_ids.reshape(windows, win_tokens)
    shift_mask = jnp.where(regions[:, :, None] == regions[:, None, :], 0.0, MASKED).astype(
        jnp.float32
    )
    mask_list = [jnp.zeros_like(shift_mask), shift_mask]
    rel_biases = [
        exact_einsum("ijm,hm->hij", one_hot, bias_table[layer_index].astype(jnp.float32))
        for layer_index in range(LAYERS)
    ]

    def scores_of(layer_index, queries, key_rows):
        return (
            mixed_einsum("bwihd,bwjhd->bwhij", queries, key_rows)
            + rel_biases[layer_index][None, None]
            + mask_list[layer_index % 2][None, :, None]
        )

    def layer_backward(layer_index, stored, grad_out):
        shifted_layer = layer_index % 2 == 1
        (
            normed_attn,
            inverse_attn,
            attn_in,
            queries,
            key_rows,
            values,
            log_total,
            mixture,
            normed_ffn,
            inverse_ffn,
            ffn_in,
            gelu_slope,
            hidden,
            stacked_qkv,
            proj_rows,
            fc1_cols,
            fc2_rows,
        ) = stored
        grad_fc2_bias = jnp.sum(grad_out, 0)
        grad_low = grad_out.astype(jnp.bfloat16)
        grad_rows = lax.all_gather(grad_low, "tensor", axis=0, tiled=True)
        grad_hidden = product(grad_rows, fc2_rows.T)
        grad_w_fc2 = product(hidden.T, grad_rows)
        grad_pre = grad_hidden * gelu_slope
        grad_pre_low = grad_pre.astype(jnp.bfloat16)
        grad_fc1_bias = jnp.sum(grad_pre, 0)
        grad_w_fc1 = product(ffn_in.T, grad_pre_low)
        grad_ffn_rows = product(grad_pre_low, fc1_cols.T)
        grad_ffn_in = lax.psum_scatter(
            grad_ffn_rows.astype(jnp.bfloat16), "tensor", scatter_dimension=0, tiled=True
        ).astype(jnp.float32)
        grad_norm2_gain = jnp.sum(grad_ffn_in * normed_ffn, 0)
        grad_norm2_bias = jnp.sum(grad_ffn_in, 0)
        grad_mid = grad_out + norm_back(
            grad_ffn_in, normed_ffn, inverse_ffn, norm2_gain[layer_index].astype(jnp.float32)
        )
        grad_proj_bias = jnp.sum(grad_mid, 0)
        grad_mid_rows = lax.all_gather(grad_mid.astype(jnp.bfloat16), "tensor", axis=0, tiled=True)
        if shifted_layer:
            grad_mid_rows = rolled(grad_mid_rows, images, -SHIFT)
        grad_mixture = product(grad_mid_rows, proj_rows.T)
        grad_w_proj = product(mixture.T, grad_mid_rows)
        grad_mixture_low = grad_mixture.astype(jnp.bfloat16).reshape(head_shape)
        scores = scores_of(layer_index, queries, key_rows)
        attention = jnp.exp(scores - log_total)
        attention_low = attention.astype(jnp.bfloat16)
        grad_values = mixed_einsum("bwhij,bwihd->bwjhd", attention_low, grad_mixture_low).reshape(
            gathered_rows, width_local
        )
        grad_attention = mixed_einsum("bwihd,bwjhd->bwhij", grad_mixture_low, values)
        row_inner = jnp.sum(attention * grad_attention, -1, keepdims=True)
        grad_scores = attention * (grad_attention - row_inner)
        grad_table = exact_einsum("ijm,hij->hm", one_hot, jnp.sum(grad_scores, (0, 1)))
        grad_scores_low = grad_scores.astype(jnp.bfloat16)
        grad_queries = (
            mixed_einsum("bwhij,bwjhd->bwihd", grad_scores_low, key_rows).reshape(
                gathered_rows, width_local
            )
            * score_scale
        )
        grad_keys = mixed_einsum("bwhij,bwihd->bwjhd", grad_scores_low, queries).reshape(
            gathered_rows, width_local
        )
        grad_qv_bias = jnp.stack([jnp.sum(grad_queries, 0), jnp.sum(grad_values, 0)])
        grad_parts = [
            grad_queries.astype(jnp.bfloat16),
            grad_keys.astype(jnp.bfloat16),
            grad_values.astype(jnp.bfloat16),
        ]
        grad_attn_rows = (
            product(grad_parts[0], stacked_qkv[0].T)
            + product(grad_parts[1], stacked_qkv[1].T)
            + product(grad_parts[2], stacked_qkv[2].T)
        )
        grad_w_qkv = jnp.stack([product(attn_in.T, grad_part) for grad_part in grad_parts])
        if shifted_layer:
            grad_attn_rows = rolled(grad_attn_rows, images, SHIFT)
        grad_attn_in = lax.psum_scatter(
            grad_attn_rows.astype(jnp.bfloat16), "tensor", scatter_dimension=0, tiled=True
        ).astype(jnp.float32)
        grad_norm1_gain = jnp.sum(grad_attn_in * normed_attn, 0)
        grad_norm1_bias = jnp.sum(grad_attn_in, 0)
        grad_in = grad_mid + norm_back(
            grad_attn_in, normed_attn, inverse_attn, norm1_gain[layer_index].astype(jnp.float32)
        )
        grad_w_qkv, grad_w_proj, grad_w_fc1, grad_w_fc2 = (
            lax.psum_scatter(
                grad_w_qkv.astype(jnp.bfloat16), "dp", scatter_dimension=1, tiled=True
            ).astype(jnp.float32),
            lax.psum_scatter(
                grad_w_proj.astype(jnp.bfloat16), "dp", scatter_dimension=1, tiled=True
            ).astype(jnp.float32),
            lax.psum_scatter(
                grad_w_fc1.astype(jnp.bfloat16), "dp", scatter_dimension=0, tiled=True
            ).astype(jnp.float32),
            lax.psum_scatter(
                grad_w_fc2.astype(jnp.bfloat16), "dp", scatter_dimension=1, tiled=True
            ).astype(jnp.float32),
        )
        return (
            grad_in,
            (
                grad_norm1_gain,
                grad_norm1_bias,
                grad_w_qkv,
                grad_qv_bias,
                grad_table,
                grad_w_proj,
                grad_proj_bias,
                grad_norm2_gain,
                grad_norm2_bias,
                grad_w_fc1,
                grad_fc1_bias,
                grad_w_fc2,
                grad_fc2_bias,
            ),
        )

    residual = inputs.astype(jnp.float32)
    forward_store = []
    for layer_index in range(LAYERS):
        layer_shifted_layer = layer_index % 2 == 1
        layer_stacked_qkv = lax.all_gather(w_qkv[layer_index], "dp", axis=1, tiled=True)
        layer_proj_rows = lax.all_gather(w_proj[layer_index], "dp", axis=1, tiled=True)
        layer_fc1_cols = lax.all_gather(w_fc1[layer_index], "dp", axis=0, tiled=True)
        layer_fc2_rows = lax.all_gather(w_fc2[layer_index], "dp", axis=1, tiled=True)
        up_bias = fc1_bias[layer_index]
        layer_normed_attn, layer_inverse_attn = normalize(residual)
        attn_local = (
            layer_normed_attn * norm1_gain[layer_index].astype(jnp.float32)
            + norm1_bias[layer_index].astype(jnp.float32)
        ).astype(jnp.bfloat16)
        layer_attn_in = lax.all_gather(attn_local, "tensor", axis=0, tiled=True)
        if layer_shifted_layer:
            layer_attn_in = rolled(layer_attn_in, images, -SHIFT)
        query_pre = product(layer_attn_in, layer_stacked_qkv[0]) + qv_bias[layer_index, 0].astype(
            jnp.float32
        )
        layer_queries = (query_pre * score_scale).astype(jnp.bfloat16).reshape(head_shape)
        layer_key_rows = (
            product(layer_attn_in, layer_stacked_qkv[1]).astype(jnp.bfloat16).reshape(head_shape)
        )
        layer_values = (
            (
                product(layer_attn_in, layer_stacked_qkv[2])
                + qv_bias[layer_index, 1].astype(jnp.float32)
            )
            .astype(jnp.bfloat16)
            .reshape(head_shape)
        )
        layer_scores = scores_of(layer_index, layer_queries, layer_key_rows)
        highest = jnp.max(layer_scores, -1, keepdims=True)
        exponent = jnp.exp(layer_scores - highest)
        denominator = jnp.sum(exponent, -1, keepdims=True)
        layer_attention = exponent / denominator
        layer_log_total = highest + jnp.log(denominator)
        layer_mixture = (
            mixed_einsum("bwhij,bwjhd->bwihd", layer_attention.astype(jnp.bfloat16), layer_values)
            .astype(jnp.bfloat16)
            .reshape(gathered_rows, width_local)
        )
        projected = product(layer_mixture, layer_proj_rows)
        if layer_shifted_layer:
            projected = rolled(projected, images, SHIFT)
        residual_mid = (
            residual
            + lax.psum_scatter(
                projected.astype(jnp.bfloat16), "tensor", scatter_dimension=0, tiled=True
            ).astype(jnp.float32)
            + proj_bias[layer_index].astype(jnp.float32)
        )
        layer_normed_ffn, layer_inverse_ffn = normalize(residual_mid)
        ffn_local = (
            layer_normed_ffn * norm2_gain[layer_index].astype(jnp.float32)
            + norm2_bias[layer_index].astype(jnp.float32)
        ).astype(jnp.bfloat16)
        layer_ffn_in = lax.all_gather(ffn_local, "tensor", axis=0, tiled=True)
        hidden_pre = product(layer_ffn_in, layer_fc1_cols) + up_bias.astype(jnp.float32)
        activated, layer_gelu_slope = gelu_parts(hidden_pre)
        layer_hidden = activated.astype(jnp.bfloat16)
        down_part = product(layer_hidden, layer_fc2_rows)
        down_sum = lax.psum_scatter(
            down_part.astype(jnp.bfloat16), "tensor", scatter_dimension=0, tiled=True
        ).astype(jnp.float32)
        residual_out = residual_mid + down_sum + fc2_bias[layer_index].astype(jnp.float32)
        layer_stored = (
            layer_normed_attn,
            layer_inverse_attn,
            layer_attn_in,
            layer_queries,
            layer_key_rows,
            layer_values,
            layer_log_total,
            layer_mixture,
            layer_normed_ffn,
            layer_inverse_ffn,
            layer_ffn_in,
            layer_gelu_slope,
            layer_hidden,
            layer_stacked_qkv,
            layer_proj_rows,
            layer_fc1_cols,
            layer_fc2_rows,
        )
        residual = residual_out
        stored = layer_stored
        forward_store.append(stored)
    grad_residual = cotangent.astype(jnp.float32)
    layer_grads = [None] * LAYERS
    for layer_index in reversed(range(LAYERS)):
        grad_residual, layer_grads[layer_index] = layer_backward(
            layer_index, forward_store[layer_index], grad_residual
        )
    stacked = [
        jnp.stack([layer_grads[layer_index][position] for layer_index in range(LAYERS)])
        for position in range(13)
    ]
    qv_total, fc1_total, table_total = lax.psum((stacked[3], stacked[10], stacked[4]), "dp")
    gain1_total, bias1_total, proj_total, gain2_total, bias2_total, fc2_total = lax.psum(
        (stacked[0], stacked[1], stacked[6], stacked[7], stacked[8], stacked[12]), ("dp", "tensor")
    )
    return (
        residual,
        grad_residual,
        gain1_total,
        bias1_total,
        stacked[2],
        qv_total,
        table_total,
        stacked[5],
        proj_total,
        gain2_total,
        bias2_total,
        stacked[9],
        fc1_total,
        stacked[11],
        fc2_total,
    )


def solution(mesh):
    in_specs = (
        P(("dp", "tensor"), None),
        P(("dp", "tensor"), None),
        P(),
        P(),
        P(),
        P(),
        P(None, None, "dp", "tensor"),
        P(None, None, "tensor"),
        P(None, "tensor", None),
        P(None, "tensor", "dp"),
        P(),
        P(),
        P(),
        P(None, "dp", "tensor"),
        P(None, "tensor"),
        P(None, "tensor", "dp"),
        P(),
    )
    out_specs = (
        P(("dp", "tensor"), None),
        P(("dp", "tensor"), None),
        P(),
        P(),
        P(None, None, "dp", "tensor"),
        P(None, None, "tensor"),
        P(None, "tensor", None),
        P(None, "tensor", "dp"),
        P(),
        P(),
        P(),
        P(None, "dp", "tensor"),
        P(None, "tensor"),
        P(None, "tensor", "dp"),
        P(),
    )
    return jax.shard_map(
        per_device, mesh=mesh, in_specs=in_specs, out_specs=out_specs, check_vma=False
    )
```

profile of v0, /device:TPU:0, one launch (start us, length us, event | category | flops | bytes accessed | tf_op | source)
XLA Modules:
  0.0 1454.6 jit_solution(11399592159413549358)
XLA Ops:
  14.0 44.0 %all-gather.1 = bf16[1,256,512]{1,2,0:T(8,128)(2,1)S(1)} all-gather(bf16[1,256,32]{1,2,0:T(8,128)(2,1)S(1)} %get-tuple-element.65), channel_id=3, replica_groups=mesh['dp'=16,'tensor'=2] {'dp'}, dimensions={2}, use_global_device_ids=true | all-gather | bytes 278528 | tf_op jit(solution)/shard_map/all_gather | solution.py:244
  58.1 40.2 %all-gather = bf16[1,3,512,256]{3,2,1,0:T(8,128)(2,1)S(1)} all-gather(bf16[1,3,32,256]{3,2,1,0:T(8,128)(2,1)S(1)} %get-tuple-element.63), channel_id=2, replica_groups=mesh['dp'=16,'tensor'=2] {'dp'}, dimensions={2}, use_global_device_ids=true | all-gather | bytes 835584 | tf_op jit(solution)/shard_map/all_gather | solution.py:243
  110.6 4.6 reshape.333
  115.2 4.9 copy.119
  123.0 4.6 reshape.334
  127.6 5.1 copy.116
  144.0 4.6 reshape.272
  152.7 6.3 reduce-scatter.17.cloned.1.call-done
  163.4 45.4 %all-gather.37.cloned.1.call-done = bf16[1,512,1024]{2,1,0:T(8,128)(2,1)} async-done(((bf16[1,32,1024]{2,1,0:T(8,128)(2,1)}), bf16[1,512,1024]{2,1,0:T(8,128)(2,1)}) %all-gather.37.cloned.1.call-update) | async-done | bytes 1048592 | tf_op jit(solution)/shard_map/all_gather | solution.py:245
  208.8 10.6 all-gather.23.cloned.1.call-done
  219.4 6.2 multiply_convert_fusion.1
  225.6 53.4 %all-gather.39.cloned.1.call-done = bf16[1,1024,512]{1,2,0:T(8,128)(2,1)} async-done(((bf16[1,1024,32]{1,2,0:T(8,128)(2,1)}), bf16[1,1024,512]{1,2,0:T(8,128)(2,1)}) %all-gather.39.cloned.1.call-update) | async-done | bytes 1048592 | tf_op jit(solution)/shard_map/all_gather | solution.py:246
  279.0 5.2 convolution_convert_fusion.3
  284.9 7.5 reduce-scatter.19.cloned.1.call-done
  296.7 42.3 %all-gather.5 = bf16[1,256,512]{1,2,0:T(8,128)(2,1)S(1)} all-gather(bf16[1,256,32]{1,2,0:T(8,128)(2,1)S(1)} %get-tuple-element.64), channel_id=7, replica_groups=mesh['dp'=16,'tensor'=2] {'dp'}, dimensions={2}, use_global_device_ids=true | all-gather | bytes 278528 | tf_op jit(solution)/shard_map/all_gather | solution.py:244
  339.2 40.4 %all-gather.4 = bf16[1,3,512,256]{3,2,1,0:T(8,128)(2,1)S(1)} all-gather(bf16[1,3,32,256]{3,2,1,0:T(8,128)(2,1)S(1)} %get-tuple-element.62), channel_id=6, replica_groups=mesh['dp'=16,'tensor'=2] {'dp'}, dimensions={2}, use_global_device_ids=true | all-gather | bytes 835584 | tf_op jit(solution)/shard_map/all_gather | solution.py:243
  398.1 4.6 reshape.338
  402.7 4.9 copy.128
  410.1 4.9 copy.130
  417.5 5.0 copy.127
  422.6 4.4 fusion.146
  433.1 7.2 copy.132
  452.1 6.2 reduce-scatter.21.cloned.1.call-done
  463.3 54.9 %all-gather.41.cloned.1.call-done = bf16[1,512,1024]{2,1,0:T(8,128)(2,1)} async-done(((bf16[1,32,1024]{2,1,0:T(8,128)(2,1)}), bf16[1,512,1024]{2,1,0:T(8,128)(2,1)}) %all-gather.41.cloned.1.call-update) | async-done | bytes 1048592 | tf_op jit(solution)/shard_map/all_gather | solution.py:245
  518.1 10.6 all-gather.27.cloned.1.call-done
  528.8 6.7 multiply_convert_fusion
  535.4 5.7 all-gather.29.cloned.1.call-done
  541.1 59.0 %all-gather.43.cloned.1.call-done = bf16[1,1024,512]{1,2,0:T(8,128)(2,1)} async-done(((bf16[1,1024,32]{1,2,0:T(8,128)(2,1)}), bf16[1,1024,512]{1,2,0:T(8,128)(2,1)}) %all-gather.43.cloned.1.call-update) | async-done | bytes 1048592 | tf_op jit(solution)/shard_map/all_gather | solution.py:246
  600.2 7.0 fusion.147
  613.1 5.0 convolution_convert_fusion.2
  622.1 10.4 reduce-scatter.23.cloned.1.call-done
  638.4 10.5 all-gather.31.cloned.1.call-done
  658.7 5.1 copy.139
  663.8 6.9 multiply_reduce_fusion.1
  670.7 4.7 bitcast_convert_fusion.2
  691.1 4.9 copy.149
  696.0 5.0 convert_element_type.366
  704.0 4.5 convert_element_type.360
  716.4 10.3 reduce-scatter.27.cloned.1.call-done
  731.8 11.1 all-gather.33.cloned.1.call-done
  742.8 6.4 fusion.148
  754.5 9.8 reduce-scatter.29.cloned.1.call-done
  770.6 5.0 convolution_convert_fusion.9
  775.7 5.9 convolution_convert_fusion.10
  781.6 5.1 fusion.90
  786.9 5.0 fusion.93
  795.4 4.6 reshape.289
  813.2 4.7 reshape.340
  818.0 4.9 copy.153
  822.9 7.3 multiply_reduce_fusion
  830.3 4.7 bitcast_convert_fusion
  843.6 4.9 convert_element_type.382
  851.5 5.2 convert_element_type.385
  863.7 4.7 convert_element_type.390
  877.0 4.6 convert_element_type.379
  894.4 38.6 %reduce-scatter.45.cloned.1.call-done = bf16[1024,32]{0,1:T(8,128)(2,1)} async-done(((bf16[1024,512]{0,1:T(8,128)(2,1)}), bf16[1024,32]{0,1:T(8,128)(2,1)}) %reduce-scatter.45.cloned.1.call-update) | async-done | bytes 65552 | tf_op jit(solution)/shard_map/reduce_scatter | solution.py:216
  934.6 75.9 %reduce-scatter.43.cloned.1.call-done = bf16[32,1024]{1,0:T(8,128)(2,1)} async-done(((bf16[512,1024]{1,0:T(8,128)(2,1)}), bf16[32,1024]{1,0:T(8,128)(2,1)}) %reduce-scatter.43.cloned.1.call-update) | async-done | bytes 65552 | tf_op jit(solution)/shard_map/reduce_scatter | solution.py:213
  1010.5 77.4 %reduce-scatter.41.cloned.1.call-done = bf16[32,1024]{1,0:T(8,128)(2,1)} async-done(((bf16[512,1024]{1,0:T(8,128)(2,1)}), bf16[32,1024]{1,0:T(8,128)(2,1)}) %reduce-scatter.41.cloned.1.call-update) | async-done | bytes 65552 | tf_op jit(solution)/shard_map/reduce_scatter | solution.py:213
  1093.6 72.5 %all-reduce.1 = (f32[2,2,256]{2,1,0:T(2,128)}, f32[2,8,169]{2,1,0:T(8,128)}, f32[2,1024]{1,0:T(2,128)}) all-reduce(f32[2,2,256]{2,1,0:T(2,128)S(1)} %pad_maximum_fusion.12, f32[2,8,169]{2,1,0:T(8,128)S(1)} %pad_maximum_fusion.8, f32[2,1024]{1,0:T(2,128)S(1)} %pad_maximum_fusion.9), channel_id=1, replica_groups=mesh['dp'=16,'tensor'=2] {'dp'}, use_global_device_ids=true, to_apply=%region_42.43 | all-reduce | flops 5776 | bytes 46208 | tf_op jit(solution)/shard_map/psum | solution.py:338
  1166.1 73.1 %reduce-scatter.37.cloned.1.call-done = bf16[256,32]{0,1:T(8,128)(2,1)} async-done(((bf16[256,512]{0,1:T(8,128)(2,1)}), bf16[256,32]{0,1:T(8,128)(2,1)}) %reduce-scatter.37.cloned.1.call-update) | async-done | bytes 16400 | tf_op jit(solution)/shard_map/reduce_scatter | solution.py:210
  1240.5 75.3 %reduce-scatter.35.cloned.1.call-done = bf16[3,32,256]{2,1,0:T(8,128)(2,1)} async-done(((bf16[3,512,256]{2,1,0:T(8,128)(2,1)}), bf16[3,32,256]{2,1,0:T(8,128)(2,1)}) %reduce-scatter.35.cloned.1.call-update) | async-done | bytes 49168 | tf_op jit(solution)/shard_map/reduce_scatter | solution.py:207
  1315.9 76.5 %reduce-scatter.33.cloned.1.call-done = bf16[3,32,256]{2,1,0:T(8,128)(2,1)} async-done(((bf16[3,512,256]{2,1,0:T(8,128)(2,1)}), bf16[3,32,256]{2,1,0:T(8,128)(2,1)}) %reduce-scatter.33.cloned.1.call-update) | async-done | bytes 49168 | tf_op jit(solution)/shard_map/reduce_scatter | solution.py:207
  1393.9 6.7 reduce-scatter.31.cloned.1.call-done
  1402.7 41.3 %all-reduce = (f32[2,512]{1,0:T(2,128)}, f32[2,512]{1,0:T(2,128)}, f32[2,512]{1,0:T(2,128)}, f32[2,512]{1,0:T(2,128)}, f32[2,512]{1,0:T(2,128)}, /*index=5*/f32[2,512]{1,0:T(2,128)}) all-reduce(f32[2,512]{1,0:T(2,128)S(1)} %pad_maximum_fusion.10, ...), channel_id=1, replica_groups=mesh['dp'=16,'tensor'=2] {'dp','tensor'}, use_global_device_ids=true, to_apply=%region_32.33 | all-reduce | flops 6144 | bytes 49152 | tf_op jit(solution)/shard_map/psum | solution.py:339
  (452 shorter events, 231.7 us)
Async XLA Ops:
  8.0 90.2 %all-gather.21.cloned.1.call-start = ((), (), s32[]{:S(2)}) async-start(), calls=%async_computation.16 | async-start | bytes 2408448 | tf_op jit(solution)/shard_map/all_gather | solution.py:253
  13.0 45.1 %copy-start.83 = (bf16[2,2,256]{2,1,0:T(2,128)(2,1)S(1)}, bf16[2,2,256]{2,1,0:T(2,128)(2,1)}, u32[]{:S(2)}) copy-start(bf16[2,2,256]{2,1,0:T(2,128)(2,1)} %param.24) | copy-start | bytes 6148
  13.0 45.1 %copy-start.70 = (bf16[2,3,32,256]{3,2,1,0:T(8,128)(2,1)S(1)}, bf16[2,3,32,256]{3,2,1,0:T(8,128)(2,1)}, u32[]{:S(2)}) copy-start(bf16[2,3,32,256]{3,2,1,0:T(8,128)(2,1)} %param.23) | copy-start | bytes 294916
  13.0 146.0 %reduce-scatter.17.cloned.1.call-start = ((), (), s32[]{:S(2)}) async-start(), calls=%async_computation.17 | async-start | bytes 2408448 | tf_op jit(solution)/shard_map/reduce_scatter | solution.py:287
  14.0 124.8 %copy-start.28 = (f32[8,49,49]{1,2,0:T(8,128)}, f32[8,49,49]{1,2,0:T(8,128)S(1)}, u32[]{:S(2)}) copy-start(f32[8,49,49]{1,2,0:T(8,128)S(1)} %copy.118) | copy-start | bytes 230500
  58.0 90.6 %copy-start.47 = (bf16[1,256,512]{1,2,0:T(8,128)(2,1)}, bf16[1,256,512]{1,2,0:T(8,128)(2,1)S(1)}, u32[]{:S(2)}) copy-start(bf16[1,256,512]{1,2,0:T(8,128)(2,1)S(1)} %all-gather.1) | copy-start | bytes 786436
  106.9 25.8 %copy-start.13 = (bf16[8,4,49,8,32]{2,4,3,1,0:T(8,128)(2,1)}, bf16[8,4,49,8,32]{2,4,3,1,0:T(8,128)(2,1)S(1)}, u32[]{:S(2)}) copy-start(bf16[8,4,49,8,32]{2,4,3,1,0:T(8,128)(2,1)S(1)} %copy.117) | copy-start | bytes 2408452
  151.6 57.1 %all-gather.37.cloned.1.call-start = ((), (), s32[]{:S(2)}) async-start(), calls=%async_computation.40 | async-start | bytes 1114112 | tf_op jit(solution)/shard_map/all_gather | solution.py:245
  152.4 67.0 %all-gather.23.cloned.1.call-start = ((), (), s32[]{:S(2)}) async-start(), calls=%async_computation.18 | async-start | bytes 2408448 | tf_op jit(solution)/shard_map/all_gather | solution.py:297
  152.7 8.4 copy-start.78
  162.6 116.4 %all-gather.39.cloned.1.call-start = ((), (), s32[]{:S(2)}) async-start(), calls=%async_computation.41 | async-start | bytes 1114112 | tf_op jit(solution)/shard_map/all_gather | solution.py:246
  163.3 129.0 %reduce-scatter.19.cloned.1.call-start = ((), (), s32[]{:S(2)}) async-start(), calls=%async_computation.19 | async-start | bytes 2408448 | tf_op jit(solution)/shard_map/reduce_scatter | solution.py:302
  284.2 95.4 %all-gather.25.cloned.1.call-start = ((), (), s32[]{:S(2)}) async-start(), calls=%async_computation.20 | async-start | bytes 2408448 | tf_op jit(solution)/shard_map/all_gather | solution.py:253
  294.0 164.3 %copy-start.5 = (f32[784,512]{1,0:T(8,128)}, f32[784,512]{1,0:T(8,128)S(1)}, u32[]{:S(2)}) copy-start(f32[784,512]{1,0:T(8,128)S(1)} %get-tuple-element.53) | copy-start | bytes 4816900
  295.6 162.7 %reduce-scatter.21.cloned.1.call-start = ((), (), s32[]{:S(2)}) async-start(), calls=%async_computation.21 | async-start | bytes 2408448 | tf_op jit(solution)/shard_map/reduce_scatter | solution.py:287
  339.1 105.4 %copy-start.49 = (bf16[1,256,512]{1,2,0:T(8,128)(2,1)}, bf16[1,256,512]{1,2,0:T(8,128)(2,1)S(1)}, u32[]{:S(2)}) copy-start(bf16[1,256,512]{1,2,0:T(8,128)(2,1)S(1)} %all-gather.5) | copy-start | bytes 786436
  379.6 17.0 %copy-start.45 = (bf16[1,3,512,256]{3,2,1,0:T(8,128)(2,1)}, bf16[1,3,512,256]{3,2,1,0:T(8,128)(2,1)S(1)}, u32[]{:S(2)}) copy-start(bf16[1,3,512,256]{3,2,1,0:T(8,128)(2,1)S(1)} %all-gather.4) | copy-start | bytes 2359300
  451.3 66.8 %all-gather.41.cloned.1.call-start = ((), (), s32[]{:S(2)}) async-start(), calls=%async_computation.42 | async-start | bytes 1114112 | tf_op jit(solution)/shard_map/all_gather | solution.py:245
  452.0 76.7 %all-gather.27.cloned.1.call-start = ((), (), s32[]{:S(2)}) async-start(), calls=%async_computation.22 | async-start | bytes 2408448 | tf_op jit(solution)/shard_map/all_gather | solution.py:297
  462.1 79.1 %all-gather.29.cloned.1.call-start = ((), (), s32[]{:S(2)}) async-start(), calls=%async_computation.24 | async-start | bytes 2408448 | tf_op jit(solution)/shard_map/all_gather | solution.py:141
  462.7 137.5 %all-gather.43.cloned.1.call-start = ((), (), s32[]{:S(2)}) async-start(), calls=%async_computation.43 | async-start | bytes 1114112 | tf_op jit(solution)/shard_map/all_gather | solution.py:246
  463.2 156.7 %reduce-scatter.25.cloned.1.call-start = ((), (), s32[]{:S(2)}) async-start(), calls=%async_computation.25 | async-start | bytes 2408448 | tf_op jit(solution)/shard_map/reduce_scatter | solution.py:149
  600.2 8.6 copy-start.96
  611.9 20.6 %reduce-scatter.23.cloned.1.call-start = ((), (), s32[]{:S(2)}) async-start(), calls=%async_computation.23 | async-start | bytes 2408448 | tf_op jit(solution)/shard_map/reduce_scatter | solution.py:302
  618.1 14.4 copy-start.40
  618.1 30.9 %all-gather.31.cloned.1.call-start = ((), (), s32[]{:S(2)}) async-start(), calls=%async_computation.26 | async-start | bytes 2408448 | tf_op jit(solution)/shard_map/all_gather | solution.py:158
  620.0 12.5 copy-start.41
  637.7 89.1 %reduce-scatter.27.cloned.1.call-start = ((), (), s32[]{:S(2)}) async-start(), calls=%async_computation.27 | async-start | bytes 2408448 | tf_op jit(solution)/shard_map/reduce_scatter | solution.py:198
  658.7 12.0 slice-start.2
  663.7 7.0 slice-start.3
  663.8 7.0 copy-start.15
  691.1 19.3 %copy-start.31 = (bf16[1568,256]{0,1:T(8,128)(2,1)}, bf16[1568,256]{0,1:T(8,128)(2,1)S(1)}, u32[]{:S(2)}) copy-start(bf16[1568,256]{0,1:T(8,128)(2,1)S(1)} %convert_element_type.363) | copy-start | bytes 2408452
  716.3 10.4 copy-start.6
  716.4 12.5 copy-start.22
  716.4 26.5 %all-gather.33.cloned.1.call-start = ((), (), s32[]{:S(2)}) async-start(), calls=%async_computation.28 | async-start | bytes 2408448 | tf_op jit(solution)/shard_map/all_gather | solution.py:141
  730.7 12.1 copy-start.95
  731.7 32.6 %reduce-scatter.29.cloned.1.call-start = ((), (), s32[]{:S(2)}) async-start(), calls=%async_computation.29 | async-start | bytes 2408448 | tf_op jit(solution)/shard_map/reduce_scatter | solution.py:149
  742.8 8.1 copy-start.94
  750.9 13.4 copy-start.69
  750.9 13.4 copy-start.74
  754.0 10.3 copy-start.3
  754.0 10.3 copy-start.12
  754.0 10.3 copy-start.79
  754.0 12.7 copy-start.24
  754.0 50.8 %all-gather.35.cloned.1.call-start = ((), (), s32[]{:S(2)}) async-start(), calls=%async_computation.30 | async-start | bytes 2408448 | tf_op jit(solution)/shard_map/all_gather | solution.py:158
  769.9 124.5 %reduce-scatter.47.cloned.1.call-start = ((), (), s32[]{:S(2)}) async-start(), calls=%async_computation.39 | async-start | bytes 1114112 | tf_op jit(solution)/shard_map/reduce_scatter | solution.py:216
  775.6 6.0 copy-start.92
  775.6 157.4 %reduce-scatter.45.cloned.1.call-start = ((), (), s32[]{:S(2)}) async-start(), calls=%async_computation.38 | async-start | bytes 1114112 | tf_op jit(solution)/shard_map/reduce_scatter | solution.py:216
  781.6 228.9 %reduce-scatter.43.cloned.1.call-start = ((), (), s32[]{:S(2)}) async-start(), calls=%async_computation.37 | async-start | bytes 1114112 | tf_op jit(solution)/shard_map/reduce_scatter | solution.py:213
  786.8 301.1 %reduce-scatter.41.cloned.1.call-start = ((), (), s32[]{:S(2)}) async-start(), calls=%async_computation.36 | async-start | bytes 1114112 | tf_op jit(solution)/shard_map/reduce_scatter | solution.py:213
  791.9 374.2 %reduce-scatter.39.cloned.1.call-start = ((), (), s32[]{:S(2)}) async-start(), calls=%async_computation.35 | async-start | bytes 278528 | tf_op jit(solution)/shard_map/reduce_scatter | solution.py:210
  803.4 435.8 %reduce-scatter.37.cloned.1.call-start = ((), (), s32[]{:S(2)}) async-start(), calls=%async_computation.34 | async-start | bytes 278528 | tf_op jit(solution)/shard_map/reduce_scatter | solution.py:210
  807.9 508.0 %reduce-scatter.35.cloned.1.call-start = ((), (), s32[]{:S(2)}) async-start(), calls=%async_computation.33 | async-start | bytes 835584 | tf_op jit(solution)/shard_map/reduce_scatter | solution.py:207
  811.0 581.4 %reduce-scatter.33.cloned.1.call-start = ((), (), s32[]{:S(2)}) async-start(), calls=%async_computation.32 | async-start | bytes 835584 | tf_op jit(solution)/shard_map/reduce_scatter | solution.py:207
  813.2 17.0 %slice-start = ((s8[7340032]{0:T(1024)(128)(4,1)}), s8[3145728]{0:T(1024)(128)(4,1)S(1)}, s32[]{:S(2)}) async-start(s8[7340032]{0:T(1024)(128)(4,1)} %bitcast.277), calls=%async_computation.44 | async-start | bytes 6291456
  822.9 7.4 slice-start.1
  822.9 7.4 copy-start.16
  873.8 526.8 %reduce-scatter.31.cloned.1.call-start = ((), (), s32[]{:S(2)}) async-start(), calls=%async_computation.31 | async-start | bytes 2408448 | tf_op jit(solution)/shard_map/reduce_scatter | solution.py:198
  893.1 196.4 %copy-start.57 = (f32[8,49,49]{1,2,0:T(8,128)S(1)}, f32[8,49,49]{1,2,0:T(8,128)}, u32[]{:S(2)}) copy-start(f32[8,49,49]{1,2,0:T(8,128)} %get-tuple-element.40) | copy-start | bytes 230500
  1089.8 310.8 %copy-start.67 = (f32[784]{0:T(1024)S(1)}, f32[784]{0:T(1024)}, u32[]{:S(2)}) copy-start(f32[784]{0:T(1024)} %copy-done.66) | copy-start | bytes 9412
  1089.8 310.8 %copy-start.72 = (f32[784]{0:T(1024)S(1)}, f32[784]{0:T(1024)}, u32[]{:S(2)}) copy-start(f32[784]{0:T(1024)} %copy-done.71) | copy-start | bytes 9412
  1089.8 310.8 %copy-start.76 = (f32[1,512]{1,0:T(1,128)S(1)}, f32[1,512]{1,0:T(1,128)}, u32[]{:S(2)}) copy-start(f32[1,512]{1,0:T(1,128)} %copy-done.75) | copy-start | bytes 6148
  1092.5 308.1 %copy-start.4 = (bf16[784,512]{1,0:T(8,128)(2,1)S(1)}, bf16[784,512]{1,0:T(8,128)(2,1)}, u32[]{:S(2)}) copy-start(bf16[784,512]{1,0:T(8,128)(2,1)} %param.17) | copy-start | bytes 2408452
  1092.5 351.5 %copy-start.20 = (f32[784,512]{1,0:T(8,128)S(1)}, f32[784,512]{1,0:T(8,128)}, u32[]{:S(2)}) copy-start(f32[784,512]{1,0:T(8,128)} %copy-done.19) | copy-start | bytes 4816900
  (72 other events, 174.7 us)
Sparse Core Ops, SparseCore 0:
  13.1 12.5 all-gather.20
  151.8 7.1 reduce-scatter.16
  284.3 7.9 reduce-scatter.18
  612.0 7.9 reduce-scatter.24
  622.1 10.3 reduce-scatter.22
  637.8 11.1 all-gather.30
  716.5 10.2 reduce-scatter.26
  770.0 11.1 all-gather.34
Sparse Core Ops, SparseCore 1:
  155.5 53.2 all-gather.36
  210.7 8.6 all-gather.22
  222.6 56.3 all-gather.38
  295.7 11.0 all-gather.24
  451.4 6.8 reduce-scatter.20
  461.7 56.4 all-gather.40
  520.1 8.6 all-gather.26
  530.2 10.9 all-gather.28
  543.8 56.3 all-gather.42
  731.8 11.0 all-gather.32
  754.1 10.1 reduce-scatter.28
  775.7 80.0 reduce-scatter.46
  857.9 75.0 reduce-scatter.44
  935.3 75.2 reduce-scatter.42
  1012.8 75.0 reduce-scatter.40
  1090.1 73.3 reduce-scatter.38
  1165.8 73.3 reduce-scatter.36
  1241.5 74.4 reduce-scatter.34
  1318.0 74.3 reduce-scatter.32
  1395.2 5.3 reduce-scatter.30
where the time goes:
time: 1460 us; the launch traced here: 1450 us
  waiting for transfers between devices  739 us (51%)
  blocking collectives  281 us (19%)
  local copies, waits for them, and re-layouts  194 us (13%)
  matrix products  157 us (11%)
  other arithmetic  64.5 us (4%)
  between operations  17.6 us (1%)
    reduce_scatter x2, waiting for transfers between devices, layer_backward(): lax.psum_scatter(grad_w_fc1.astype(jnp.bfloat16), 'dp', scatter_dimension...  153 us
    reduce_scatter x2, waiting for transfers between devices, layer_backward(): lax.psum_scatter(grad_w_qkv.astype(jnp.bfloat16), 'dp', scatter_dimension...  152 us
    all_gather x2, waiting for transfers between devices, per_device(): lax.all_gather(w_fc2[layer_index], 'dp', axis=1, tiled=True)  112 us
    dot_general x36, matrix products, product(): jnp.dot(first_operand, second_operand, preferred_element_type=jnp.float32)  106 us
    all_gather x2, waiting for transfers between devices, per_device(): lax.all_gather(w_fc1[layer_index], 'dp', axis=0, tiled=True)  100 us
    all_gather x2, blocking collectives, per_device(): lax.all_gather(w_proj[layer_index], 'dp', axis=1, tiled=True)  86.3 us
    all_gather x2, blocking collectives, per_device(): lax.all_gather(w_qkv[layer_index], 'dp', axis=1, tiled=True)  80.6 us
    reduce_scatter x2, waiting for transfers between devices, layer_backward(): lax.psum_scatter(grad_w_proj.astype(jnp.bfloat16), 'dp', scatter_dimensio...  73.1 us
  transfers between devices with their start and end apart: 28, of which 23 were waited for; matrix products, arithmetic and copies ran while one was open for 11% of the time, Pallas kernels for 0%

commit v1 on v0

v1 whole, which is shorter than its diff:
```python
import functools

import jax
import jax.numpy as jnp
from jax import lax
from jax.experimental import pallas as pl
from jax.experimental.pallas import tpu as pltpu
from jax.sharding import PartitionSpec as P

HD = 32
GRID = 14
WIN = 7
SHIFT = 3
LAYERS = 2
TABLE = 169
EPS = 1e-05
MASKED = -100.0
PADDED = -1e30
SLOT = 64
LANES = 128
EXACT_PRECISION = lax.Precision.HIGHEST
F32 = jnp.float32
BF16 = jnp.bfloat16


def normalize(residual):
    average = jnp.mean(residual, -1, keepdims=True)
    centered = residual - average
    inverse = lax.rsqrt(jnp.mean(centered * centered, -1, keepdims=True) + EPS)
    return (centered * inverse, inverse)


def norm_back(grad_out, normed, inverse, gain_value):
    scaled = grad_out * gain_value
    return inverse * (
        scaled
        - jnp.mean(scaled, -1, keepdims=True)
        - normed * jnp.mean(scaled * normed, -1, keepdims=True)
    )


def gelu_parts(hidden_pre):
    cumulative = 0.5 * (1.0 + lax.erf(hidden_pre * 0.7071067811865476))
    density = jnp.exp(-0.5 * hidden_pre * hidden_pre) * 0.3989422804014327
    return (hidden_pre * cumulative, cumulative + hidden_pre * density)


def dot(a, b, ca=1, cb=0):
    return lax.dot_general(a, b, (((ca,), (cb,)), ((), ())), preferred_element_type=F32)


def stack_heads(block, masks):
    return jnp.concatenate([block * m for m in masks], axis=0)


def merge_heads(stacked, masks):
    total = None
    for h, m in enumerate(masks):
        part = stacked[h * SLOT : (h + 1) * SLOT] * m
        total = part if total is None else total + part
    return total


def head_masks(dtype):
    lane = lax.broadcasted_iota(jnp.int32, (SLOT, LANES), 1)
    return [
        jnp.where((lane >= h * HD) & (lane < (h + 1) * HD), 1.0, 0.0).astype(dtype)
        for h in range(LANES // HD)
    ]


def probabilities(queries_stacked, keys, bias):
    scores = dot(queries_stacked, keys, 1, 1) + bias
    exponent = jnp.exp(scores - jnp.max(scores, -1, keepdims=True))
    return exponent / jnp.sum(exponent, -1, keepdims=True)


def attention_kernel(qkv_ref, bias_ref, mask_ref, out_ref):
    width = out_ref.shape[1]
    low, full = head_masks(BF16), head_masks(F32)
    mask = jnp.concatenate([mask_ref[0]] * len(low), axis=0)
    for g in range(width // LANES):
        q = qkv_ref[:, g * LANES : (g + 1) * LANES]
        k = qkv_ref[:, width + g * LANES : width + (g + 1) * LANES]
        v = qkv_ref[:, 2 * width + g * LANES : 2 * width + (g + 1) * LANES]
        attention = probabilities(stack_heads(q, low), k, bias_ref[g] + mask)
        mixed = dot(attention.astype(BF16), v)
        out_ref[:, g * LANES : (g + 1) * LANES] = merge_heads(mixed, full).astype(BF16)


def attention_back_kernel(scale, qkv_ref, dmix_ref, bias_ref, mask_ref, dqkv_ref, dscore_ref, dbias_ref):
    width = dmix_ref.shape[1]
    low, full = head_masks(BF16), head_masks(F32)
    mask = jnp.concatenate([mask_ref[0]] * len(low), axis=0)

    @pl.when(pl.program_id(0) == 0)
    def _():
        dscore_ref[...] = jnp.zeros_like(dscore_ref)
        dbias_ref[...] = jnp.zeros_like(dbias_ref)

    def put(part, g, value):
        at = slice(part * width + g * LANES, part * width + (g + 1) * LANES)
        dqkv_ref[:, at] = value.astype(BF16)
        if part != 1:
            rows = value[0:8]
            for r in range(1, SLOT // 8):
                rows = rows + value[r * 8 : (r + 1) * 8]
            dbias_ref[:, at] += rows

    for g in range(width // LANES):
        q = qkv_ref[:, g * LANES : (g + 1) * LANES]
        k = qkv_ref[:, width + g * LANES : width + (g + 1) * LANES]
        v = qkv_ref[:, 2 * width + g * LANES : 2 * width + (g + 1) * LANES]
        dm = dmix_ref[:, g * LANES : (g + 1) * LANES]
        q_stacked = stack_heads(q, low)
        dm_stacked = stack_heads(dm, low)
        attention = probabilities(q_stacked, k, bias_ref[g] + mask)
        dattention = dot(dm_stacked, v, 1, 1)
        inner = jnp.sum(attention * dattention, -1, keepdims=True)
        dscores = attention * (dattention - inner)
        dscore_ref[g] += dscores
        dl = dscores.astype(BF16)
        put(0, g, merge_heads(dot(dl, k), full) * scale)
        put(1, g, dot(dl, q_stacked, 0, 0))
        put(2, g, dot(attention.astype(BF16), dm_stacked, 0, 0))


def attention_forward(qkv, bias, mask):
    rows, width = qkv.shape[0], qkv.shape[1] // 3
    windows = mask.shape[0]
    return pl.pallas_call(
        attention_kernel,
        grid=(rows // SLOT,),
        out_shape=jax.ShapeDtypeStruct((rows, width), BF16),
        in_specs=[
            pl.BlockSpec((SLOT, 3 * width), lambda i: (i, 0)),
            pl.BlockSpec(bias.shape, lambda i: (0, 0, 0)),
            pl.BlockSpec((1, SLOT, SLOT), lambda i: (lax.rem(i, windows), 0, 0)),
        ],
        out_specs=pl.BlockSpec((SLOT, width), lambda i: (i, 0)),
        cost_estimate=pl.CostEstimate(
            flops=rows * width * SLOT * 16, bytes_accessed=rows * width * 8, transcendentals=rows * width * 2
        ),
        name="attention_forward",
    )(qkv, bias, mask)


def attention_backward(qkv, dmix, bias, mask, scale):
    rows, width = dmix.shape
    windows = mask.shape[0]
    return pl.pallas_call(
        functools.partial(attention_back_kernel, scale),
        grid=(rows // SLOT,),
        out_shape=(
            jax.ShapeDtypeStruct((rows, 3 * width), BF16),
            jax.ShapeDtypeStruct(bias.shape, F32),
            jax.ShapeDtypeStruct((8, 3 * width), F32),
        ),
        in_specs=[
            pl.BlockSpec((SLOT, 3 * width), lambda i: (i, 0)),
            pl.BlockSpec((SLOT, width), lambda i: (i, 0)),
            pl.BlockSpec(bias.shape, lambda i: (0, 0, 0)),
            pl.BlockSpec((1, SLOT, SLOT), lambda i: (lax.rem(i, windows), 0, 0)),
        ],
        out_specs=(
            pl.BlockSpec((SLOT, 3 * width), lambda i: (i, 0)),
            pl.BlockSpec(bias.shape, lambda i: (0, 0, 0)),
            pl.BlockSpec((8, 3 * width), lambda i: (0, 0)),
        ),
        cost_estimate=pl.CostEstimate(
            flops=rows * width * SLOT * 40, bytes_accessed=rows * width * 16, transcendentals=rows * width * 2
        ),
        name="attention_backward",
    )(qkv, dmix, bias, mask)


def placement(tokens, shift):
    per_side = GRID // WIN
    slots = tokens // (WIN * WIN) * SLOT
    row = lax.broadcasted_iota(jnp.int32, (slots, tokens), 0)
    column = lax.broadcasted_iota(jnp.int32, (slots, tokens), 1)
    window, p = row // SLOT, row % SLOT
    image, w = window // (per_side * per_side), window % (per_side * per_side)
    gi = (w // per_side * WIN + p // WIN + shift) % GRID
    gj = (w % per_side * WIN + p % WIN + shift) % GRID
    source = (
        image * (GRID * GRID)
        + (gi // WIN * per_side + gj // WIN) * (WIN * WIN)
        + gi % WIN * WIN
        + gj % WIN
    )
    return ((column == source) & (p < WIN * WIN)).astype(BF16)


def pack_weights(w_qkv, w_proj, w_fc1, w_fc2):
    rows = w_qkv.shape[1]
    return jnp.concatenate(
        [w_qkv.transpose(1, 0, 2).reshape(rows, -1), w_proj.T, w_fc1, w_fc2.T], axis=1
    )


def per_device(
    inputs,
    cotangent,
    region_ids,
    rel_index,
    norm1_gain,
    norm1_bias,
    w_qkv,
    qv_bias,
    bias_table,
    w_proj,
    proj_bias,
    norm2_gain,
    norm2_bias,
    w_fc1,
    fc1_bias,
    w_fc2,
    fc2_bias,
):
    n_dp, n_t = lax.axis_size("dp"), lax.axis_size("tensor")
    t_index = lax.axis_index("tensor")
    tokens, width = inputs.shape
    ff_local = fc1_bias.shape[1]
    heads_local = bias_table.shape[1]
    heads = heads_local * n_t
    local = heads_local * HD
    shard = width // n_dp
    cuts = (3 * local, 4 * local, 4 * local + ff_local, 4 * local + 2 * ff_local)
    per_side = GRID // WIN
    windows = per_side * per_side
    win_tokens = WIN * WIN
    score_scale = HD ** (-0.5)
    groups = width // LANES

    def pack_grads(g_qkv, g_proj, g_fc1, g_fc2):
        pieces = []
        for g, n in ((g_qkv, 3), (g_proj, 1), (g_fc1, 1), (g_fc2, 1)):
            shaped = g.astype(BF16).reshape(n_dp, shard, n, n_t, -1)
            pieces.append(shaped.transpose(0, 3, 1, 2, 4).reshape(n_dp, n_t, shard, -1))
        return jnp.concatenate(pieces, -1)

    small = jnp.concatenate([qv_bias.reshape(-1), fc1_bias.reshape(-1), bias_table.reshape(-1)])
    extra = -(-small.shape[0] // (shard * LANES)) * LANES
    small_packed = jnp.pad(small, (0, shard * extra - small.shape[0])).reshape(shard, extra)

    def gather_layer(l):
        packed = pack_weights(w_qkv[l], w_proj[l], w_fc1[l], w_fc2[l])
        if l == 0:
            packed = jnp.concatenate([packed, small_packed], axis=1)
        whole = gather_shards(packed)
        parts = []
        lo = 0
        for n, hi in zip((3, 1, 1, 1), cuts):
            piece = whole[..., lo:hi].reshape(n_dp, n_t, shard, n, (hi - lo) // n)
            parts.append(piece.transpose(0, 2, 3, 1, 4).reshape(width, -1))
            lo = hi
        return parts, whole[0, :, :, lo:].reshape(n_t, -1)

    gathered = [gather_layer(l) for l in range(LAYERS)]
    weights = [parts for parts, _ in gathered]
    small = gathered[0][1][:, : small.shape[0]]
    n_qv, n_fc = qv_bias.size, fc1_bias.size
    qv_full = small[:, :n_qv].reshape(n_t, LAYERS, 2, local).transpose(1, 2, 0, 3).reshape(LAYERS, 2, width)
    fc1_full = small[:, n_qv : n_qv + n_fc].reshape(n_t, LAYERS, ff_local).transpose(1, 0, 2).reshape(LAYERS, -1)
    table_full = (
        small[:, n_qv + n_fc :].reshape(n_t, LAYERS, heads_local, TABLE).transpose(1, 0, 2, 3).reshape(LAYERS, heads, TABLE)
    ).astype(F32)
    fc1_full = fc1_full.astype(F32)
    qv_full = qv_full.astype(F32)

    pad = SLOT - win_tokens
    index_padded = jnp.pad(rel_index, ((0, pad), (0, pad)), constant_values=-1).reshape(-1)
    one_hot = (index_padded[None, :] == jnp.arange(TABLE, dtype=jnp.int32)[:, None]).astype(F32)
    regions = region_ids.reshape(windows, win_tokens)
    shift_mask = jnp.where(regions[:, :, None] == regions[:, None, :], 0.0, MASKED).astype(F32)

    def padded_mask(mask):
        return jnp.pad(
            jnp.pad(mask, ((0, 0), (0, pad), (0, 0))), ((0, 0), (0, 0), (0, pad)), constant_values=PADDED
        )

    masks = [padded_mask(jnp.zeros_like(shift_mask)), padded_mask(shift_mask)]
    biases = [
        jnp.dot(table_full[l], one_hot, precision=EXACT_PRECISION).reshape(groups, LANES // HD * SLOT, SLOT)
        for l in range(LAYERS)
    ]
    places = [placement(tokens, SHIFT * (l % 2)) for l in range(LAYERS)]
    scale_row = jnp.concatenate([jnp.full((width,), score_scale, F32), jnp.ones((2 * width,), F32)])

    residual = inputs.astype(F32)
    store = []
    for l in range(LAYERS):
        qkv_w, proj_w, fc1_w, fc2_w = weights[l]
        place = places[l]
        normed1, inverse1 = normalize(residual)
        attn_in = (normed1 * norm1_gain[l].astype(F32) + norm1_bias[l].astype(F32)).astype(BF16)
        attn_pad = dot(place, attn_in).astype(BF16)
        qkv_bias = jnp.concatenate([qv_full[l, 0], jnp.zeros((width,), F32), qv_full[l, 1]])
        qkv = ((dot(attn_pad, qkv_w) + qkv_bias) * scale_row).astype(BF16)
        mixture = dot(place, attention_forward(qkv, biases[l], masks[l % 2]), 0, 0).astype(BF16)
        residual_mid = residual + dot(mixture, proj_w, 1, 1) + proj_bias[l].astype(F32)
        normed2, inverse2 = normalize(residual_mid)
        ffn_in = (normed2 * norm2_gain[l].astype(F32) + norm2_bias[l].astype(F32)).astype(BF16)
        activated, slope = gelu_parts(dot(ffn_in, fc1_w) + fc1_full[l])
        hidden = activated.astype(BF16)
        slope = slope.astype(BF16)
        store.append((normed1, inverse1, attn_in, qkv, mixture, normed2, inverse2, ffn_in, slope, hidden))
        residual = residual_mid + dot(hidden, fc2_w, 1, 1) + fc2_bias[l].astype(F32)

    g = cotangent.astype(F32)
    weight_grads = [None] * LAYERS
    small_grads = [None] * LAYERS
    for l in reversed(range(LAYERS)):
        qkv_w, proj_w, fc1_w, fc2_w = weights[l]
        place = places[l]
        normed1, inverse1, attn_in, qkv, mixture, normed2, inverse2, ffn_in, slope, hidden = store[l]
        g_fc2_bias = jnp.sum(g, 0)
        gl = g.astype(BF16)
        dpre = dot(gl, fc2_w) * slope.astype(F32)
        dpl = dpre.astype(BF16)
        g_fc1_bias = jnp.sum(dpre, 0)
        g_fc2 = dot(gl, hidden, 0, 0)
        g_fc1 = dot(ffn_in, dpl, 0, 0)
        dffn = dot(dpl, fc1_w, 1, 1)
        g_n2_gain = jnp.sum(dffn * normed2, 0)
        g_n2_bias = jnp.sum(dffn, 0)
        g_mid = g + norm_back(dffn, normed2, inverse2, norm2_gain[l].astype(F32))
        g_proj_bias = jnp.sum(g_mid, 0)
        gm = g_mid.astype(BF16)
        g_proj = dot(gm, mixture, 0, 0)
        dmix = dot(gm, proj_w).astype(BF16)
        dmix_pad = dot(place, dmix).astype(BF16)
        dqkv_pad, dscores, dbias = attention_backward(qkv, dmix_pad, biases[l], masks[l % 2], score_scale)
        g_table = lax.dot_general(
            dscores.reshape(heads, SLOT * SLOT), one_hot, (((1,), (1,)), ((), ())), precision=EXACT_PRECISION
        )
        dqkv = dot(place, dqkv_pad, 0, 0).astype(BF16)
        g_qkv = dot(attn_in, dqkv, 0, 0)
        dattn = dot(dqkv, qkv_w, 1, 1)
        g_n1_gain = jnp.sum(dattn * normed1, 0)
        g_n1_bias = jnp.sum(dattn, 0)
        g = g_mid + norm_back(dattn, normed1, inverse1, norm1_gain[l].astype(F32))
        dbias_rows = jnp.sum(dbias, 0)
        weight_grads[l] = reduce_shards(pack_grads(g_qkv, g_proj, g_fc1, g_fc2)).astype(F32)
        small_grads[l] = [
            g_n1_gain, g_n1_bias, g_proj_bias, g_n2_gain, g_n2_bias, g_fc2_bias,
            dbias_rows[:width], dbias_rows[2 * width :], g_fc1_bias, g_table.reshape(-1),
        ]

    flat = jnp.concatenate([v for l in range(LAYERS) for v in small_grads[l]])
    total = sum_everywhere(flat).reshape(LAYERS, -1)
    vectors = total[:, : 6 * width].reshape(LAYERS, 6, width)
    at = 6 * width
    qv_total = total[:, at : at + 2 * width].reshape(LAYERS, 2, width)
    qv_total = lax.dynamic_slice_in_dim(qv_total, t_index * local, local, 2)
    at += 2 * width
    fc1_total = lax.dynamic_slice_in_dim(total[:, at : at + ff_local * n_t], t_index * ff_local, ff_local, 1)
    at += ff_local * n_t
    table_total = lax.dynamic_slice_in_dim(
        total[:, at:].reshape(LAYERS, heads, TABLE), t_index * heads_local, heads_local, 1
    )
    grads = jnp.stack(weight_grads)
    qkv_total = grads[..., : cuts[0]].reshape(LAYERS, shard, 3, local).transpose(0, 2, 1, 3)
    proj_w_total = grads[..., cuts[0] : cuts[1]].transpose(0, 2, 1)
    fc1_w_total = grads[..., cuts[1] : cuts[2]]
    fc2_w_total = grads[..., cuts[2] :].transpose(0, 2, 1)
    return (
        residual,
        g,
        vectors[:, 0],
        vectors[:, 1],
        qkv_total,
        qv_total,
        table_total,
        proj_w_total,
        vectors[:, 2],
        vectors[:, 3],
        vectors[:, 4],
        fc1_w_total,
        fc1_total,
        fc2_w_total,
        vectors[:, 5],
    )


def gather_shards(packed):
    n_dp, n_t = lax.axis_size("dp"), lax.axis_size("tensor")
    rows = lax.all_gather(packed, ("dp", "tensor"), axis=0, tiled=False)
    return rows.reshape((n_dp, n_t) + packed.shape)


def reduce_shards(packed):
    rows = packed.reshape((-1,) + packed.shape[2:])
    return lax.psum_scatter(rows, ("dp", "tensor"), scatter_dimension=0, tiled=False)


def partners():
    found = []
    for axis in ("tensor", "dp"):
        size, bit = lax.axis_size(axis), 1
        assert size & (size - 1) == 0
        me = lax.axis_index(axis)
        while bit < size:
            found.append((axis, me + bit - 2 * bit * ((me // bit) % 2)))
            bit *= 2
    return found


def exchange_kernel(x_ref, out_ref, held, arrived, send_sem, recv_sem):
    steps = partners()
    barrier = pltpu.get_barrier_semaphore()
    for axis, place in steps:
        pl.semaphore_signal(barrier, inc=1, device_id={axis: place}, device_id_type=pl.DeviceIdType.MESH)
    pl.semaphore_wait(barrier, len(steps))
    for s, (axis, place) in enumerate(steps):
        source = x_ref if s == 0 else held.at[s - 1]
        copy = pltpu.make_async_remote_copy(
            src_ref=source,
            dst_ref=arrived.at[s],
            send_sem=send_sem.at[s],
            recv_sem=recv_sem.at[s],
            device_id={axis: place},
            device_id_type=pl.DeviceIdType.MESH,
        )
        copy.start()
        copy.wait()
        total = source[...] + arrived[s]
        if s < len(steps) - 1:
            held[s] = total
        else:
            out_ref[...] = total


def sum_everywhere(flat):
    size = flat.shape[0]
    rows = -(-size // (8 * LANES)) * 8
    x = jnp.pad(flat, (0, rows * LANES - size)).reshape(rows, LANES)
    n = len(partners())
    total = pl.pallas_call(
        exchange_kernel,
        out_shape=jax.ShapeDtypeStruct(x.shape, F32),
        in_specs=[pl.BlockSpec(memory_space=pltpu.VMEM)],
        out_specs=pl.BlockSpec(memory_space=pltpu.VMEM),
        scratch_shapes=[
            pltpu.VMEM((n,) + x.shape, F32),
            pltpu.VMEM((n,) + x.shape, F32),
            pltpu.SemaphoreType.DMA((n,)),
            pltpu.SemaphoreType.DMA((n,)),
        ],
        compiler_params=pltpu.CompilerParams(collective_id=0, has_side_effects=True),
        name="sum_everywhere",
    )(x)
    return total.reshape(-1)[:size]


def solution(mesh):
    in_specs = (
        P(("dp", "tensor"), None),
        P(("dp", "tensor"), None),
        P(),
        P(),
        P(),
        P(),
        P(None, None, "dp", "tensor"),
        P(None, None, "tensor"),
        P(None, "tensor", None),
        P(None, "tensor", "dp"),
        P(),
        P(),
        P(),
        P(None, "dp", "tensor"),
        P(None, "tensor"),
        P(None, "tensor", "dp"),
        P(),
    )
    out_specs = (
        P(("dp", "tensor"), None),
        P(("dp", "tensor"), None),
        P(),
        P(),
        P(None, None, "dp", "tensor"),
        P(None, None, "tensor"),
        P(None, "tensor", None),
        P(None, "tensor", "dp"),
        P(),
        P(),
        P(),
        P(None, "dp", "tensor"),
        P(None, "tensor"),
        P(None, "tensor", "dp"),
        P(),
    )
    return jax.shard_map(
        per_device, mesh=mesh, in_specs=in_specs, out_specs=out_specs, check_vma=False
    )
```

time: 1460 us -> 659 us (0.45)
  waiting for transfers between devices: 739 us -> 203 us
  blocking collectives: 281 us -> 0 us
  Pallas kernels: 0 us -> 117 us
  local copies, waits for them, and re-layouts: 194 us -> 148 us
  other arithmetic: 64.5 us -> 28.9 us
  matrix products: 157 us -> 135 us
    reduce_scatter x16 -> x2, waiting for transfers between devices: 476 us -> 105 us  [reduce_shards(): lax.psum_scatter(rows, ('dp', 'tensor'), scatter_dimension=0, tiled=False)]
    all_gather x4 -> x0, blocking collectives: 167 us -> none  [the longest x2 86.3 us: per_device(): lax.all_gather(w_proj[layer_index], 'dp', axis=1, tiled=True)]
    all_gather x12 -> x2, waiting for transfers between devices: 261 us -> 97.8 us  [gather_shards(): rows = lax.all_gather(packed, ('dp', 'tensor'), axis=0, tiled=False)]
    pallas_call x0 -> x5, Pallas kernels: none -> 117 us  [the longest x2 63.5 us: attention_backward(): pl.pallas_call(functools.partial(attention_back_kernel, scale), grid=(row...]
    psum x2 -> x0, blocking collectives: 114 us -> none  [the longest x1 72.5 us: per_device(): lax.psum((stacked[3], stacked[10], stacked[4]), 'dp')]
    convert_element_type x21 -> x3, local copies, waits for them, and re-layouts: 74.6 us -> 4.04 us  [the longest x1 3.99 us: pack_grads(): shaped = g.astype(BF16).reshape(n_dp, shard, n, n_t, -1)]
    reshape x23 -> x30, local copies, waits for them, and re-layouts: 88.1 us -> 59.1 us  [the longest x10 33.2 us: pack_grads(): shaped = g.astype(BF16).reshape(n_dp, shard, n, n_t, -1)]
    reduce_sum x14 -> x5, other arithmetic: 32.6 us -> 4.3 us  [the longest x2 2.54 us: per_device(): g_proj_bias = jnp.sum(g_mid, 0)]
  transfers between devices with their start and end apart: 28 -> 4, of which waited for: 23 -> 3; matrix products, arithmetic and copies ran while one was open for 11% -> 18% of each run, Pallas kernels for 0% -> 8%
where the time goes in v1:
time: 659 us; the launch traced here: 648 us
  waiting for transfers between devices  203 us (31%)
  local copies, waits for them, and re-layouts  148 us (22%)
  matrix products  135 us (20%)
  Pallas kernels  117 us (18%)
  other arithmetic  28.9 us (4%)
  between operations  15.4 us (2%)
    dot_general x32, matrix products, dot(): lax.dot_general(a, b, (((ca,), (cb,)), ((), ())), preferred_element_type=...  128 us
    reduce_scatter x2, waiting for transfers between devices, reduce_shards(): lax.psum_scatter(rows, ('dp', 'tensor'), scatter_dimension=0, tiled=False)  105 us
    all_gather x2, waiting for transfers between devices, gather_shards(): rows = lax.all_gather(packed, ('dp', 'tensor'), axis=0, tiled=False)  97.8 us
    pallas_call x2, Pallas kernels, attention_backward(): pl.pallas_call(functools.partial(attention_back_kernel, scale), grid=(row...  63.5 us
    reshape x10, local copies, waits for them, and re-layouts, pack_grads(): shaped = g.astype(BF16).reshape(n_dp, shard, n, n_t, -1)  33.2 us
    pallas_call x2, Pallas kernels, attention_forward(): pl.pallas_call(attention_kernel, grid=(rows // SLOT,), out_shape=jax.Shap...  33 us
    unnamed x214, local copies, waits for them, and re-layouts  29.9 us
    pallas_call x1, Pallas kernels, sum_everywhere(): pl.pallas_call(exchange_kernel, out_shape=jax.ShapeDtypeStruct(x.shape, F...  20.5 us
  transfers between devices with their start and end apart: 4, of which 3 were waited for; matrix products, arithmetic and copies ran while one was open for 18% of the time, Pallas kernels for 8%

profile of v1, /device:TPU:0, one launch (start us, length us, event | category | flops | bytes accessed | tf_op | source)
XLA Modules:
  0.0 648.1 jit_solution(5393898507134662171)
XLA Ops:
  24.1 5.8 convolution_convert_fusion.11.clone.4
  30.0 53.4 %all-gather.7.cloned.1.call-done = bf16[1024,3072]{1,0:T(8,128)(2,1)} async-done(((bf16[32,3072]{1,0:T(8,128)(2,1)}), bf16[1024,3072]{1,0:T(8,128)(2,1)}) %all-gather.7.cloned.1.call-update) | async-done | bytes 6291472 | tf_op jit(solution)/shard_map/all_gather | solution.py:389
  84.6 2.9 slice.260
  90.9 2.2 copy.87
  95.0 4.3 reshape.317
  99.3 3.6 copy.68
  102.9 5.0 reshape.318
  108.0 2.2 copy.86
  112.1 44.3 %all-gather.5.cloned.1.call-done = bf16[1024,3328]{1,0:T(8,128)(2,1)} async-done(((bf16[32,3328]{1,0:T(8,128)(2,1)}), bf16[1024,3328]{1,0:T(8,128)(2,1)}) %all-gather.5.cloned.1.call-update) | async-done | bytes 6815760 | tf_op jit(solution)/shard_map/all_gather | solution.py:389
  161.0 2.7 slice.248
  163.6 4.2 fusion.128
  173.1 2.2 copy.84
  177.3 4.2 reshape.305
  181.5 3.6 copy.63
  185.1 4.3 reshape.306
  189.4 5.2 multiply_convert_fusion.3.qkv_ref
  194.6 16.4 %attention_forward.2 = bf16[1024,512]{1,0:T(8,128)(2,1)} custom-call(bf16[1024,1536]{1,0:T(8,128)(2,1)} %multiply_convert_fusion.3.qkv_ref, f32[4,256,64]{2,1,0:T(8,128)} %reshape.308.bias_ref, f32[4,64,64]{2,1,0:T(8,128)} %fusion.88.mask_ref), custom_call_target="tpu_custom_call" | custom-call | flops 536870912 | bytes 4194304 | tf_op jit(solution)/shard_map/attention_forward/pallas_call | solution.py:131
  211.0 5.7 convolution_convert_fusion.13
  219.1 2.2 copy.83
  221.9 5.1 multiply_convert_fusion.1
  229.6 4.9 convolution_convert_fusion.10.clone.4
  234.5 3.5 multiply_convert_fusion.2.qkv_ref
  238.0 16.6 %attention_forward.3 = bf16[1024,512]{1,0:T(8,128)(2,1)} custom-call(bf16[1024,1536]{1,0:T(8,128)(2,1)} %multiply_convert_fusion.2.qkv_ref, f32[4,256,64]{2,1,0:T(8,128)} %reshape.319.bias_ref, f32[4,64,64]{2,1,0:T(8,128)} %pad_select_fusion.mask_ref), custom_call_target="tpu_custom_call" | custom-call | flops 536870912 | bytes 4194304 | tf_op jit(solution)/shard_map/attention_forward/pallas_call | solution.py:131
  254.7 5.9 convolution_convert_fusion.12
  264.2 6.6 %fusion.16 = (f32[2048]{0:T(1024)}, bf16[784,2048]{1,0:T(8,128)(2,1)S(1)}, bf16[784,2048]{1,0:T(8,128)(2,1)}, f32[2048,784]{0,1:T(8,128)S(1)}) fusion(f32[784,2048]{1,0:T(8,128)S(1)} %fusion.112, f32[2048]{0:T(1024)S(1)} %bitcast.298, bf16[784,512]{1,0:T(8,128)(2,1)S(1)} %copy-done.23, bf16[512,2048]{1,0:T(8,128)(2,1)S(1)} %bitcast.255), kind=kOutput, calls=%fused_computation.58 | convolution fusion | flops 1668249600 | bytes 22183936 | tf_op jit(solution)/shard_map/dot_general | solution.py:49
  270.8 2.8 multiply_reduce_fusion
  273.6 4.1 convolution_convert_fusion.3
  281.3 6.9 %convolution_convert_fusion.9.dmix_ref = bf16[1024,512]{1,0:T(8,128)(2,1)} fusion(s32[1024]{0:T(1024)S(1)} %get-tuple-element.138, s32[1024]{0:T(1024)S(1)} %get-tuple-element.139, pred[1024]{0:T(1024)(128)(4,1)S(1)} %get-tuple-element.141, s32[1024]{0:T(1024)S(1)} %get-tuple-element.137, s32[1024]{0:T(1024)S(1)} %get-tuple-element.140, ...), kind=kOutput, calls=%fused_computation.165 | convolution fusion | flops 906903552 | bytes 1869824 | tf_op jit(solution)/shard_map/dot_general | solution.py:49
  288.1 31.8 %attention_backward.2 = (bf16[1024,1536]{1,0:T(8,128)(2,1)}, f32[4,256,64]{2,1,0:T(8,128)}, f32[8,1536]{1,0:T(8,128)}) custom-call(bf16[1024,1536]{1,0:T(8,128)(2,1)} %multiply_convert_fusion.2.qkv_ref, bf16[1024,512]{1,0:T(8,128)(2,1)} %convolution_convert_fusion.9.dmix_ref, f32[4,256,64]{2,1,0:T(8,128)} %reshape.319.bias_ref, ...), custom_call_target="tpu_custom_call" | custom-call | flops 1342177280 | bytes 8388608 | tf_op jit(solution)/shard_map/attention_backward/pallas_call | solution.py:151
  320.0 8.0 %convolution_convert_fusion.1 = bf16[784,1536]{1,0:T(8,128)(2,1)S(1)} fusion(bf16[1024,1536]{1,0:T(8,128)(2,1)} %get-tuple-element.21, s32[1024]{0:T(1024)S(1)} %get-tuple-element.138, s32[1024]{0:T(1024)S(1)} %get-tuple-element.139, pred[1024]{0:T(1024)(128)(4,1)S(1)} %get-tuple-element.141, s32[1024]{0:T(1024)S(1)} %get-tuple-element.137, ...), kind=kOutput, calls=%fused_computation.107 | convolution fusion | flops 2551750656 | bytes 5572608 | tf_op jit(solution)/shard_map/dot_general | solution.py:49
  328.0 2.4 multiply_reduce_fusion.1
  330.5 3.1 convolution_convert_fusion.6
  335.5 3.8 convolution_convert_fusion.4
  339.4 4.8 fusion.14
  344.2 2.8 multiply_reduce_fusion.2
  347.1 4.2 convolution_convert_fusion.5
  355.5 3.8 fusion.58
  360.3 4.0 copy.79
  364.2 4.5 reshape.341
  368.7 3.6 copy.80
  372.3 4.5 reshape.340
  376.8 3.6 copy.78
  380.5 3.6 reshape.338
  384.1 4.6 reshape.337
  388.6 3.6 copy.75
  392.2 2.5 copy.102
  394.7 4.3 concatenate.53
  398.9 5.7 pad_maximum_fusion.1
  405.9 4.7 reshape.336
  410.7 3.7 copy.74
  414.4 6.8 %convolution_convert_fusion.8.dmix_ref = bf16[1024,512]{1,0:T(8,128)(2,1)} fusion(s32[1024]{0:T(1024)S(1)} %get-tuple-element.138, s32[1024]{0:T(1024)S(1)} %get-tuple-element.139, pred[1024]{0:T(1024)(128)(4,1)S(1)} %get-tuple-element.141, s32[1024]{0:T(1024)S(1)} %get-tuple-element.137, s32[1024]{0:T(1024)S(1)} %get-tuple-element.140, ...), kind=kOutput, calls=%fused_computation.164 | convolution fusion | flops 905297920 | bytes 1869824 | tf_op jit(solution)/shard_map/dot_general | solution.py:49
  421.2 31.7 %attention_backward.3 = (bf16[1024,1536]{1,0:T(8,128)(2,1)}, f32[4,256,64]{2,1,0:T(8,128)}, f32[8,1536]{1,0:T(8,128)}) custom-call(bf16[1024,1536]{1,0:T(8,128)(2,1)} %multiply_convert_fusion.3.qkv_ref, bf16[1024,512]{1,0:T(8,128)(2,1)} %convolution_convert_fusion.8.dmix_ref, f32[4,256,64]{2,1,0:T(8,128)} %reshape.308.bias_ref, f32[4,64,64]{2,1,0:T(8,128)} %fusion.88.mask_ref), custom_call_target="tpu_custom_call" | custom-call | flops 1342177280 | bytes 8388608 | tf_op jit(solution)/shard_map/attention_backward/pallas_call | solution.py:151
  452.9 8.3 %convolution_convert_fusion = bf16[784,1536]{1,0:T(8,128)(2,1)S(1)} fusion(bf16[1024,1536]{1,0:T(8,128)(2,1)} %get-tuple-element.22, s32[1024]{0:T(1024)S(1)} %get-tuple-element.138, s32[1024]{0:T(1024)S(1)} %get-tuple-element.139, pred[1024]{0:T(1024)(128)(4,1)S(1)} %get-tuple-element.141, s32[1024]{0:T(1024)S(1)} %get-tuple-element.137, ...), kind=kOutput, calls=%fused_computation.106 | convolution fusion | flops 2550145024 | bytes 5572608 | tf_op jit(solution)/shard_map/dot_general | solution.py:49
  462.7 3.1 convolution_convert_fusion.7
  465.8 4.8 reshape.334
  470.6 3.9 copy.103
  474.6 5.3 concatenate.48
  479.9 6.3 pad_maximum_fusion
  488.4 2.3 fusion.54
  494.2 5.0 fusion.72
  500.0 20.5 %sum_everywhere.1 = f32[144,128]{1,0:T(8,128)} custom-call(f32[144,128]{1,0:T(8,128)} %pad_bitcast_fusion.x_ref), custom_call_target="tpu_custom_call" | custom-call | tf_op jit(solution)/shard_map/sum_everywhere/pallas_call | solution.py:440
  524.2 3.4 fusion.71
  527.6 5.0 add_add_fusion
  532.6 105.3 %reduce-scatter.3.cloned.1.call-done = bf16[1,32,3072]{2,1,0:T(8,128)(2,1)} async-done(((bf16[32,32,3072]{2,1,0:T(8,128)(2,1)}), bf16[1,32,3072]{2,1,0:T(8,128)(2,1)}) %reduce-scatter.3.cloned.1.call-update) | async-done | bytes 196624 | tf_op jit(solution)/shard_map/reduce_scatter | solution.py:395
  (327 shorter events, 72.4 us)
Async XLA Ops:
  7.2 14.0 %copy-start.9 = (bf16[784,512]{1,0:T(8,128)(2,1)S(1)}, bf16[784,512]{1,0:T(8,128)(2,1)}, u32[]{:S(2)}) copy-start(bf16[784,512]{1,0:T(8,128)(2,1)} %param.17) | copy-start | bytes 2408452
  7.2 14.5 %copy-start.64 = (bf16[2,512]{1,0:T(2,128)(2,1)S(1)}, bf16[2,512]{1,0:T(2,128)(2,1)}, u32[]{:S(2)}) copy-start(bf16[2,512]{1,0:T(2,128)(2,1)} %param.21) | copy-start | bytes 6148
  7.2 14.5 %copy-start.65 = (bf16[2,512]{1,0:T(2,128)(2,1)S(1)}, bf16[2,512]{1,0:T(2,128)(2,1)}, u32[]{:S(2)}) copy-start(bf16[2,512]{1,0:T(2,128)(2,1)} %param.22) | copy-start | bytes 6148
  7.2 14.5 %copy-start.66 = (bf16[2,512]{1,0:T(2,128)(2,1)S(1)}, bf16[2,512]{1,0:T(2,128)(2,1)}, u32[]{:S(2)}) copy-start(bf16[2,512]{1,0:T(2,128)(2,1)} %param.27) | copy-start | bytes 6148
  7.2 15.1 %copy-start.67 = (bf16[2,512]{1,0:T(2,128)(2,1)S(1)}, bf16[2,512]{1,0:T(2,128)(2,1)}, u32[]{:S(2)}) copy-start(bf16[2,512]{1,0:T(2,128)(2,1)} %param.28) | copy-start | bytes 6148
  7.2 15.7 %copy-start.68 = (bf16[2,512]{1,0:T(2,128)(2,1)S(1)}, bf16[2,512]{1,0:T(2,128)(2,1)}, u32[]{:S(2)}) copy-start(bf16[2,512]{1,0:T(2,128)(2,1)} %param.29) | copy-start | bytes 6148
  7.2 16.3 %copy-start.69 = (bf16[2,512]{1,0:T(2,128)(2,1)S(1)}, bf16[2,512]{1,0:T(2,128)(2,1)}, u32[]{:S(2)}) copy-start(bf16[2,512]{1,0:T(2,128)(2,1)} %param.33) | copy-start | bytes 6148
  7.3 76.2 %all-gather.7.cloned.1.call-start = ((), (), s32[]{:S(2)}) async-start(), calls=%async_computation.5 | async-start | bytes 6488064 | tf_op jit(solution)/shard_map/all_gather | solution.py:389
  11.3 145.1 %all-gather.5.cloned.1.call-start = ((), (), s32[]{:S(2)}) async-start(), calls=%async_computation.4 | async-start | bytes 7028736 | tf_op jit(solution)/shard_map/all_gather | solution.py:389
  16.7 515.9 %reduce-scatter.5.cloned.1.call-start = ((), (), s32[]{:S(2)}) async-start(), calls=%async_computation.3 | async-start | bytes 6488064 | tf_op jit(solution)/shard_map/reduce_scatter | solution.py:395
  18.4 140.2 %copy-start.49 = (s32[4096]{0:T(1024)}, s32[4096]{0:T(1024)S(1)}, u32[]{:S(2)}) copy-start(s32[4096]{0:T(1024)S(1)} %eq.66) | copy-start | bytes 49156
  21.7 8.3 %copy-start.52 = (f32[1,512]{1,0:T(1,128)}, f32[1,512]{1,0:T(1,128)S(1)}, u32[]{:S(2)}) copy-start(f32[1,512]{1,0:T(1,128)S(1)} %get-tuple-element.118) | copy-start | bytes 6148
  21.7 207.8 %copy-start.60 = (f32[1,512]{1,0:T(1,128)}, f32[1,512]{1,0:T(1,128)S(1)}, u32[]{:S(2)}) copy-start(f32[1,512]{1,0:T(1,128)S(1)} %get-tuple-element.117) | copy-start | bytes 6148
  21.7 8.2 %copy-start.80 = (f32[1,512]{1,0:T(1,128)}, f32[1,512]{1,0:T(1,128)S(1)}, u32[]{:S(2)}) copy-start(f32[1,512]{1,0:T(1,128)S(1)} %get-tuple-element.120) | copy-start | bytes 6148
  21.8 207.8 %copy-start.84 = (f32[1,512]{1,0:T(1,128)}, f32[1,512]{1,0:T(1,128)S(1)}, u32[]{:S(2)}) copy-start(f32[1,512]{1,0:T(1,128)S(1)} %get-tuple-element.119) | copy-start | bytes 6148
  22.9 198.9 %copy-start.43 = (f32[1,512]{1,0:T(1,128)}, f32[1,512]{1,0:T(1,128)S(1)}, u32[]{:S(2)}) copy-start(f32[1,512]{1,0:T(1,128)S(1)} %get-tuple-element.112) | copy-start | bytes 6148
  23.5 198.3 %copy-start.82 = (f32[1,512]{1,0:T(1,128)}, f32[1,512]{1,0:T(1,128)S(1)}, u32[]{:S(2)}) copy-start(f32[1,512]{1,0:T(1,128)S(1)} %get-tuple-element.114) | copy-start | bytes 6148
  24.1 5.8 copy-start.46
  83.4 5.6 copy-start.11
  102.9 5.0 copy-start.5
  168.5 53.3 %copy-start.70 = (f32[1,2,1024]{2,0,1:T(1,128)}, f32[1,2,1024]{2,0,1:T(1,128)S(1)}, u32[]{:S(2)}) copy-start(f32[1,2,1024]{2,0,1:T(1,128)S(1)} %get-tuple-element.100) | copy-start | bytes 24580
  173.1 43.7 %copy-start.17 = (bf16[64,8,2,256]{3,1,2,0:T(8,128)(2,1)}, bf16[64,8,2,256]{3,1,2,0:T(8,128)(2,1)S(1)}, u32[]{:S(2)}) copy-start(bf16[64,8,2,256]{3,1,2,0:T(8,128)(2,1)S(1)} %copy.93) | copy-start | bytes 1572868
  181.5 7.9 %copy-start.87 = (f32[1536]{0:T(1024)S(1)}, f32[1536]{0:T(1024)}, u32[]{:S(2)}) copy-start(f32[1536]{0:T(1024)} %constant.197.clone.1) | copy-start | bytes 18436
  189.3 5.3 copy-start.19
  217.5 9.5 %copy-start.2 = (f32[784,512]{1,0:T(8,128)}, f32[784,512]{1,0:T(8,128)S(1)}, u32[]{:S(2)}) copy-start(f32[784,512]{1,0:T(8,128)S(1)} %get-tuple-element.124) | copy-start | bytes 4816900
  221.8 5.2 copy-start.7
  221.9 5.2 copy-start.15
  229.2 5.3 copy-start.39
  229.5 5.0 copy-start.50
  254.7 6.0 copy-start.12
  254.7 6.0 copy-start.55
  261.3 16.4 %copy-start = (f32[784,512]{1,0:T(8,128)}, f32[784,512]{1,0:T(8,128)S(1)}, u32[]{:S(2)}) copy-start(f32[784,512]{1,0:T(8,128)S(1)} %get-tuple-element.130) | copy-start | bytes 4816900
  319.9 8.1 %copy-start.21 = (bf16[512,1536]{1,0:T(8,128)(2,1)S(1)}, bf16[512,1536]{1,0:T(8,128)(2,1)}, u32[]{:S(2)}) copy-start(bf16[512,1536]{1,0:T(8,128)(2,1)} %reshape.318) | copy-start | bytes 4718596
  319.9 8.1 %copy-start.40 = (f32[784]{0:T(1024)S(1)}, f32[784]{0:T(1024)}, u32[]{:S(2)}) copy-start(f32[784]{0:T(1024)} %copy-done.39) | copy-start | bytes 9412
  319.9 8.1 %copy-start.51 = (f32[784]{0:T(1024)S(1)}, f32[784]{0:T(1024)}, u32[]{:S(2)}) copy-start(f32[784]{0:T(1024)} %copy-done.50) | copy-start | bytes 9412
  320.0 8.1 %copy-start.61 = (f32[1,512]{1,0:T(1,128)S(1)}, f32[1,512]{1,0:T(1,128)}, u32[]{:S(2)}) copy-start(f32[1,512]{1,0:T(1,128)} %copy-done.60) | copy-start | bytes 6148
  330.5 8.8 %slice-start = ((s8[6422528]{0:T(1024)(128)(4,1)}), s8[4194304]{0:T(1024)(128)(4,1)S(1)}, s32[]{:S(2)}) async-start(s8[6422528]{0:T(1024)(128)(4,1)} %bitcast.316), calls=%async_computation.6 | async-start | bytes 8388608
  333.6 5.7 slice-start.1
  404.7 233.2 %reduce-scatter.3.cloned.1.call-start = ((), (), s32[]{:S(2)}) async-start(), calls=%async_computation.2 | async-start | bytes 6488064 | tf_op jit(solution)/shard_map/reduce_scatter | solution.py:395
  405.9 8.5 %copy-start.22 = (bf16[784,512]{1,0:T(8,128)(2,1)S(1)}, bf16[784,512]{1,0:T(8,128)(2,1)}, u32[]{:S(2)}) copy-start(bf16[784,512]{1,0:T(8,128)(2,1)} %convolution_convert_fusion.14.clone.5) | copy-start | bytes 2408452
  452.9 9.8 %copy-start.10 = (bf16[784,512]{1,0:T(8,128)(2,1)S(1)}, bf16[784,512]{1,0:T(8,128)(2,1)}, u32[]{:S(2)}) copy-start(bf16[784,512]{1,0:T(8,128)(2,1)} %param.17) | copy-start | bytes 2408452
  452.9 9.8 %copy-start.37 = (f32[784]{0:T(1024)S(1)}, f32[784]{0:T(1024)}, u32[]{:S(2)}) copy-start(f32[784]{0:T(1024)} %copy-done.36) | copy-start | bytes 9412
  452.9 9.8 %copy-start.47 = (f32[784]{0:T(1024)S(1)}, f32[784]{0:T(1024)}, u32[]{:S(2)}) copy-start(f32[784]{0:T(1024)} %copy-done.46) | copy-start | bytes 9412
  452.9 9.8 %copy-start.53 = (f32[1,512]{1,0:T(1,128)S(1)}, f32[1,512]{1,0:T(1,128)}, u32[]{:S(2)}) copy-start(f32[1,512]{1,0:T(1,128)} %copy-done.52) | copy-start | bytes 6148
  452.9 9.8 %copy-start.81 = (f32[1,512]{1,0:T(1,128)S(1)}, f32[1,512]{1,0:T(1,128)}, u32[]{:S(2)}) copy-start(f32[1,512]{1,0:T(1,128)} %copy-done.80) | copy-start | bytes 6148
  494.1 5.1 copy-start.56
  494.1 5.1 copy-start.57
  494.1 5.1 copy-start.58
  494.1 5.1 copy-start.59
  494.1 5.1 copy-start.62
  494.1 5.1 copy-start.63
  494.1 5.1 copy-start.73
  494.1 5.1 copy-start.74
  494.1 5.1 copy-start.75
  494.1 5.1 copy-start.76
  494.2 5.1 copy-start.77
  494.2 5.1 copy-start.78
  494.2 30.0 %copy-start.38 = (f32[784]{0:T(1024)S(1)}, f32[784]{0:T(1024)}, u32[]{:S(2)}) copy-start(f32[784]{0:T(1024)} %copy-done.36) | copy-start | bytes 9412
  494.2 30.0 %copy-start.48 = (f32[784]{0:T(1024)S(1)}, f32[784]{0:T(1024)}, u32[]{:S(2)}) copy-start(f32[784]{0:T(1024)} %copy-done.46) | copy-start | bytes 9412
  494.2 30.0 %copy-start.54 = (f32[1,512]{1,0:T(1,128)S(1)}, f32[1,512]{1,0:T(1,128)}, u32[]{:S(2)}) copy-start(f32[1,512]{1,0:T(1,128)} %copy-done.52) | copy-start | bytes 6148
  499.2 28.4 %copy-start.1 = (f32[784,512]{1,0:T(8,128)S(1)}, f32[784,512]{1,0:T(8,128)}, u32[]{:S(2)}) copy-start(f32[784,512]{1,0:T(8,128)} %copy-done) | copy-start | bytes 4816900
  499.2 28.4 %copy-start.79 = (f32[1,512]{1,0:T(1,128)S(1)}, f32[1,512]{1,0:T(1,128)}, u32[]{:S(2)}) copy-start(f32[1,512]{1,0:T(1,128)} %get-tuple-element.109) | copy-start | bytes 6148
  521.7 5.9 copy-start.14
  532.6 108.1 %copy-start.25 = (bf16[1,32,3072]{2,1,0:T(8,128)(2,1)S(1)}, bf16[1,32,3072]{2,1,0:T(8,128)(2,1)}, u32[]{:S(2)}) copy-start(bf16[1,32,3072]{2,1,0:T(8,128)(2,1)} %reduce-scatter.5.cloned.1.call-done) | copy-start | bytes 589828
  (36 other events, 103.8 us)
Sparse Core Ops, SparseCore 0:
  11.5 71.8 all-gather.6
  86.8 69.5 all-gather.4
  404.8 114.2 reduce-scatter.4
  524.6 113.2 reduce-scatter.2

commit v2 on v1

--- a/solution.py
+++ b/solution.py
@@ -1,4 +1,5 @@
 import functools
+import itertools
 
 import jax
 import jax.numpy as jnp
@@ -17,6 +18,7 @@
 MASKED = -100.0
 PADDED = -1e30
 SLOT = 64
+PER_STEP = 2
 LANES = 128
 EXACT_PRECISION = lax.Precision.HIGHEST
 F32 = jnp.float32
@@ -72,46 +74,48 @@
 def probabilities(queries_stacked, keys, bias):
     scores = dot(queries_stacked, keys, 1, 1) + bias
     exponent = jnp.exp(scores - jnp.max(scores, -1, keepdims=True))
-    return exponent / jnp.sum(exponent, -1, keepdims=True)
+    return exponent * (1.0 / jnp.sum(exponent, -1, keepdims=True))
 
 
 def attention_kernel(qkv_ref, bias_ref, mask_ref, out_ref):
     width = out_ref.shape[1]
     low, full = head_masks(BF16), head_masks(F32)
-    mask = jnp.concatenate([mask_ref[0]] * len(low), axis=0)
-    for g in range(width // LANES):
-        q = qkv_ref[:, g * LANES : (g + 1) * LANES]
-        k = qkv_ref[:, width + g * LANES : width + (g + 1) * LANES]
-        v = qkv_ref[:, 2 * width + g * LANES : 2 * width + (g + 1) * LANES]
+    for g, w in itertools.product(range(width // LANES), range(mask_ref.shape[0])):
+        rows = slice(w * SLOT, (w + 1) * SLOT)
+        mask = jnp.concatenate([mask_ref[w]] * len(low), axis=0)
+        q = qkv_ref[rows, g * LANES : (g + 1) * LANES]
+        k = qkv_ref[rows, width + g * LANES : width + (g + 1) * LANES]
+        v = qkv_ref[rows, 2 * width + g * LANES : 2 * width + (g + 1) * LANES]
         attention = probabilities(stack_heads(q, low), k, bias_ref[g] + mask)
         mixed = dot(attention.astype(BF16), v)
-        out_ref[:, g * LANES : (g + 1) * LANES] = merge_heads(mixed, full).astype(BF16)
+        out_ref[rows, g * LANES : (g + 1) * LANES] = merge_heads(mixed, full).astype(BF16)
 
 
 def attention_back_kernel(scale, qkv_ref, dmix_ref, bias_ref, mask_ref, dqkv_ref, dscore_ref, dbias_ref):
     width = dmix_ref.shape[1]
     low, full = head_masks(BF16), head_masks(F32)
-    mask = jnp.concatenate([mask_ref[0]] * len(low), axis=0)
 
     @pl.when(pl.program_id(0) == 0)
     def _():
         dscore_ref[...] = jnp.zeros_like(dscore_ref)
         dbias_ref[...] = jnp.zeros_like(dbias_ref)
 
-    def put(part, g, value):
+    def put(part, g, at_rows, value):
         at = slice(part * width + g * LANES, part * width + (g + 1) * LANES)
-        dqkv_ref[:, at] = value.astype(BF16)
+        dqkv_ref[at_rows, at] = value.astype(BF16)
         if part != 1:
             rows = value[0:8]
             for r in range(1, SLOT // 8):
                 rows = rows + value[r * 8 : (r + 1) * 8]
             dbias_ref[:, at] += rows
 
-    for g in range(width // LANES):
-        q = qkv_ref[:, g * LANES : (g + 1) * LANES]
-        k = qkv_ref[:, width + g * LANES : width + (g + 1) * LANES]
-        v = qkv_ref[:, 2 * width + g * LANES : 2 * width + (g + 1) * LANES]
-        dm = dmix_ref[:, g * LANES : (g + 1) * LANES]
+    for g, w in itertools.product(range(width // LANES), range(mask_ref.shape[0])):
+        rows = slice(w * SLOT, (w + 1) * SLOT)
+        mask = jnp.concatenate([mask_ref[w]] * len(low), axis=0)
+        q = qkv_ref[rows, g * LANES : (g + 1) * LANES]
+        k = qkv_ref[rows, width + g * LANES : width + (g + 1) * LANES]
+        v = qkv_ref[rows, 2 * width + g * LANES : 2 * width + (g + 1) * LANES]
+        dm = dmix_ref[rows, g * LANES : (g + 1) * LANES]
         q_stacked = stack_heads(q, low)
         dm_stacked = stack_heads(dm, low)
         attention = probabilities(q_stacked, k, bias_ref[g] + mask)
@@ -120,9 +124,9 @@
         dscores = attention * (dattention - inner)
         dscore_ref[g] += dscores
         dl = dscores.astype(BF16)
-        put(0, g, merge_heads(dot(dl, k), full) * scale)
-        put(1, g, dot(dl, q_stacked, 0, 0))
-        put(2, g, dot(attention.astype(BF16), dm_stacked, 0, 0))
+        put(0, g, rows, merge_heads(dot(dl, k), full) * scale)
+        put(1, g, rows, dot(dl, q_stacked, 0, 0))
+        put(2, g, rows, dot(attention.astype(BF16), dm_stacked, 0, 0))
 
 
 def attention_forward(qkv, bias, mask):
@@ -130,14 +134,14 @@
     windows = mask.shape[0]
     return pl.pallas_call(
         attention_kernel,
-        grid=(rows // SLOT,),
+        grid=(rows // (PER_STEP * SLOT),),
         out_shape=jax.ShapeDtypeStruct((rows, width), BF16),
         in_specs=[
-            pl.BlockSpec((SLOT, 3 * width), lambda i: (i, 0)),
+            pl.BlockSpec((PER_STEP * SLOT, 3 * width), lambda i: (i, 0)),
             pl.BlockSpec(bias.shape, lambda i: (0, 0, 0)),
-            pl.BlockSpec((1, SLOT, SLOT), lambda i: (lax.rem(i, windows), 0, 0)),
+            pl.BlockSpec((PER_STEP, SLOT, SLOT), lambda i: (lax.rem(i, windows // PER_STEP), 0, 0)),
         ],
-        out_specs=pl.BlockSpec((SLOT, width), lambda i: (i, 0)),
+        out_specs=pl.BlockSpec((PER_STEP * SLOT, width), lambda i: (i, 0)),
         cost_estimate=pl.CostEstimate(
             flops=rows * width * SLOT * 16, bytes_accessed=rows * width * 8, transcendentals=rows * width * 2
         ),
@@ -150,20 +154,20 @@
     windows = mask.shape[0]
     return pl.pallas_call(
         functools.partial(attention_back_kernel, scale),
-        grid=(rows // SLOT,),
+        grid=(rows // (PER_STEP * SLOT),),
         out_shape=(
             jax.ShapeDtypeStruct((rows, 3 * width), BF16),
             jax.ShapeDtypeStruct(bias.shape, F32),
             jax.ShapeDtypeStruct((8, 3 * width), F32),
         ),
         in_specs=[
-            pl.BlockSpec((SLOT, 3 * width), lambda i: (i, 0)),
-            pl.BlockSpec((SLOT, width), lambda i: (i, 0)),
+            pl.BlockSpec((PER_STEP * SLOT, 3 * width), lambda i: (i, 0)),
+            pl.BlockSpec((PER_STEP * SLOT, width), lambda i: (i, 0)),
             pl.BlockSpec(bias.shape, lambda i: (0, 0, 0)),
-            pl.BlockSpec((1, SLOT, SLOT), lambda i: (lax.rem(i, windows), 0, 0)),
+            pl.BlockSpec((PER_STEP, SLOT, SLOT), lambda i: (lax.rem(i, windows // PER_STEP), 0, 0)),
         ],
         out_specs=(
-            pl.BlockSpec((SLOT, 3 * width), lambda i: (i, 0)),
+            pl.BlockSpec((PER_STEP * SLOT, 3 * width), lambda i: (i, 0)),
             pl.BlockSpec(bias.shape, lambda i: (0, 0, 0)),
             pl.BlockSpec((8, 3 * width), lambda i: (0, 0)),
         ),
@@ -234,11 +238,14 @@
     groups = width // LANES
 
     def pack_grads(g_qkv, g_proj, g_fc1, g_fc2):
-        pieces = []
-        for g, n in ((g_qkv, 3), (g_proj, 1), (g_fc1, 1), (g_fc2, 1)):
-            shaped = g.astype(BF16).reshape(n_dp, shard, n, n_t, -1)
-            pieces.append(shaped.transpose(0, 3, 1, 2, 4).reshape(n_dp, n_t, shard, -1))
-        return jnp.concatenate(pieces, -1)
+        sides = []
+        for t in range(n_t):
+            pieces = []
+            for g, n in ((g_qkv, 3), (g_proj, 1), (g_fc1, 1), (g_fc2, 1)):
+                step = g.shape[1] // (n * n_t)
+                pieces += [g[:, (m * n_t + t) * step : (m * n_t + t + 1) * step].astype(BF16) for m in range(n)]
+            sides.append(jnp.concatenate(pieces, axis=1).reshape(n_dp, shard, -1))
+        return jnp.stack(sides, axis=1)
 
     small = jnp.concatenate([qv_bias.reshape(-1), fc1_bias.reshape(-1), bias_table.reshape(-1)])
     extra = -(-small.shape[0] // (shard * LANES)) * LANES
@@ -249,16 +256,23 @@
         if l == 0:
             packed = jnp.concatenate([packed, small_packed], axis=1)
         whole = gather_shards(packed)
+        return whole, whole[0, :, :, cuts[3] :].reshape(n_t, -1)
+
+    def unpack_weights(whole):
+        blocks = [whole[:, t].reshape(width, -1) for t in range(n_t)]
         parts = []
         lo = 0
         for n, hi in zip((3, 1, 1, 1), cuts):
-            piece = whole[..., lo:hi].reshape(n_dp, n_t, shard, n, (hi - lo) // n)
-            parts.append(piece.transpose(0, 2, 3, 1, 4).reshape(width, -1))
+            step = (hi - lo) // n
+            parts.append(
+                jnp.concatenate([b[:, lo + m * step : lo + (m + 1) * step] for m in range(n) for b in blocks], axis=1)
+            )
             lo = hi
-        return parts, whole[0, :, :, lo:].reshape(n_t, -1)
+        return parts
 
     gathered = [gather_layer(l) for l in range(LAYERS)]
-    weights = [parts for parts, _ in gathered]
+    wholes = [whole for whole, _ in gathered]
+    weights = [None] * LAYERS
     small = gathered[0][1][:, : small.shape[0]]
     n_qv, n_fc = qv_bias.size, fc1_bias.size
     qv_full = small[:, :n_qv].reshape(n_t, LAYERS, 2, local).transpose(1, 2, 0, 3).reshape(LAYERS, 2, width)
@@ -291,6 +305,8 @@
     residual = inputs.astype(F32)
     store = []
     for l in range(LAYERS):
+        whole, residual = lax.optimization_barrier((wholes[l], residual)) if l else (wholes[l], residual)
+        weights[l] = unpack_weights(whole)
         qkv_w, proj_w, fc1_w, fc2_w = weights[l]
         place = places[l]
         normed1, inverse1 = normalize(residual)

time: 659 us -> 595 us (0.903)
  local copies, waits for them, and re-layouts: 148 us -> 62.5 us
  waiting for transfers between devices: 203 us -> 251 us
  Pallas kernels: 117 us -> 106 us
  other arithmetic: 28.9 us -> 18.8 us
    reduce_scatter x2, waiting for transfers between devices: 105 us -> 166 us  [reduce_shards(): lax.psum_scatter(rows, ('dp', 'tensor'), scatter_dimension=0, tiled=False)]
    reshape x14 -> x0, local copies, waits for them, and re-layouts: 51 us -> none  [the longest x10 33.2 us: pack_grads(): shaped = g.astype(BF16).reshape(n_dp, shard, n, n_t, -1)]
    transpose x8 -> x0, local copies, waits for them, and re-layouts: 22.7 us -> none  [the longest x6 15.6 us: pack_grads(): pieces.append(shaped.transpose(0, 3, 1, 2, 4).reshape(n_dp, n_t, shard, -1))]
    all_gather x2, waiting for transfers between devices: 97.8 us -> 84.8 us  [gather_shards(): rows = lax.all_gather(packed, ('dp', 'tensor'), axis=0, tiled=False)]
    concatenate x2 -> x0, other arithmetic: 12 us -> none  [pack_grads(): return jnp.concatenate(pieces, -1)]
    pallas_call x2, Pallas kernels: 33 us -> 22.9 us  [attention_forward(): pl.pallas_call(attention_kernel, grid=(rows // (PER_STEP * SLOT),), out_s...]
    concatenate x2, local copies, waits for them, and re-layouts: 9.58 us -> 0.4 us  [pack_grads(): sides.append(jnp.concatenate(pieces, axis=1).reshape(n_dp, shard, -1))]
    unnamed x214 -> x278, local copies, waits for them, and re-layouts: 29.9 us -> 25.9 us
  transfers between devices with their start and end apart: 4 -> 4, of which waited for: 3 -> 4; matrix products, arithmetic and copies ran while one was open for 18% -> 14% of each run, Pallas kernels for 8% -> 6%
where the time goes in v2:
time: 595 us; the launch traced here: 586 us
  waiting for transfers between devices  251 us (42%)
  matrix products  132 us (22%)
  Pallas kernels  106 us (18%)
  local copies, waits for them, and re-layouts  62.5 us (11%)
  other arithmetic  18.8 us (3%)
  between operations  16 us (3%)
    reduce_scatter x2, waiting for transfers between devices, reduce_shards(): lax.psum_scatter(rows, ('dp', 'tensor'), scatter_dimension=0, tiled=False)  166 us
    dot_general x32, matrix products, dot(): lax.dot_general(a, b, (((ca,), (cb,)), ((), ())), preferred_element_type=...  127 us
    all_gather x2, waiting for transfers between devices, gather_shards(): rows = lax.all_gather(packed, ('dp', 'tensor'), axis=0, tiled=False)  84.8 us
    pallas_call x2, Pallas kernels, attention_backward(): pl.pallas_call(functools.partial(attention_back_kernel, scale), grid=(row...  60 us
    unnamed x278, local copies, waits for them, and re-layouts  25.9 us
    pallas_call x1, Pallas kernels, sum_everywhere(): pl.pallas_call(exchange_kernel, out_shape=jax.ShapeDtypeStruct(x.shape, F...  23 us
    pallas_call x2, Pallas kernels, attention_forward(): pl.pallas_call(attention_kernel, grid=(rows // (PER_STEP * SLOT),), out_s...  22.9 us
  transfers between devices with their start and end apart: 4, of which 4 were waited for; matrix products, arithmetic and copies ran while one was open for 14% of the time, Pallas kernels for 6%

profile of v2, /device:TPU:0, one launch (start us, length us, event | category | flops | bytes accessed | tf_op | source)
XLA Modules:
  0.0 586.4 jit_solution(12777843991983515158)
XLA Ops:
  17.6 1.4 convert_reduce_fusion
  18.9 1.5 fusion.73
  21.3 5.8 convolution_convert_fusion.11.clone.4
  30.4 57.0 %all-gather.7.cloned.1.call-done = bf16[1024,3328]{1,0:T(8,128)(2,1)} async-done(((bf16[32,3328]{1,0:T(8,128)(2,1)}), bf16[1024,3328]{1,0:T(8,128)(2,1)}) %all-gather.7.cloned.1.call-update) | async-done | bytes 6815760 | tf_op jit(solution)/shard_map/all_gather | solution.py:405
  89.0 1.0 reshape.216.bias_ref
  90.0 3.5 fusion.143
  93.6 1.6 copy-done.6
  96.7 1.1 copy-done.50
  97.8 3.5 multiply_convert_fusion.3.qkv_ref
  101.3 11.3 %attention_forward.2 = bf16[1024,512]{1,0:T(8,128)(2,1)} custom-call(bf16[1024,1536]{1,0:T(8,128)(2,1)} %multiply_convert_fusion.3.qkv_ref, f32[4,256,64]{2,1,0:T(8,128)} %reshape.216.bias_ref, f32[4,64,64]{2,1,0:T(8,128)} %fusion.93.mask_ref), custom_call_target="tpu_custom_call" | custom-call | flops 536870912 | bytes 4194304 | tf_op jit(solution)/shard_map/attention_forward/pallas_call | solution.py:135
  112.7 5.8 convolution_convert_fusion.13
  119.8 1.3 fusion.56
  122.2 5.0 multiply_convert_fusion.1
  127.3 1.7 copy-done.112
  128.9 1.9 add_add_fusion.2
  130.8 27.7 %all-gather.5.cloned.1.call-done = bf16[1024,3072]{1,0:T(8,128)(2,1)} async-done(((bf16[32,3072]{1,0:T(8,128)(2,1)}), bf16[1024,3072]{1,0:T(8,128)(2,1)}) %all-gather.5.cloned.1.call-update) | async-done | bytes 6291472 | tf_op jit(solution)/shard_map/all_gather | solution.py:405
  158.5 5.1 fusion.144
  164.4 1.0 copy-done.8
  165.4 1.2 fusion.149
  166.6 1.2 reshape.217.bias_ref
  168.4 3.1 fusion.150
  174.4 1.1 fusion.151
  175.5 1.1 fusion.152
  176.6 5.1 convolution_convert_fusion.10.clone.4
  181.7 3.5 multiply_convert_fusion.2.qkv_ref
  185.3 11.6 %attention_forward.3 = bf16[1024,512]{1,0:T(8,128)(2,1)} custom-call(bf16[1024,1536]{1,0:T(8,128)(2,1)} %multiply_convert_fusion.2.qkv_ref, f32[4,256,64]{2,1,0:T(8,128)} %reshape.217.bias_ref, f32[4,64,64]{2,1,0:T(8,128)} %pad_select_fusion.mask_ref), custom_call_target="tpu_custom_call" | custom-call | flops 536870912 | bytes 4194304 | tf_op jit(solution)/shard_map/attention_forward/pallas_call | solution.py:135
  196.9 5.8 convolution_convert_fusion.12
  204.8 1.9 fusion.81
  206.8 6.5 %fusion.16 = (f32[2048]{0:T(1024)}, bf16[784,2048]{1,0:T(8,128)(2,1)S(1)}, bf16[784,2048]{1,0:T(8,128)(2,1)}, f32[2048,784]{0,1:T(8,128)S(1)}) fusion(f32[784,2048]{1,0:T(8,128)S(1)} %fusion.81, f32[2048]{0:T(1024)S(1)} %bitcast.206, bf16[784,512]{1,0:T(8,128)(2,1)S(1)} %copy-done.37, bf16[512,1024]{1,0:T(8,128)(2,1)S(1)} %copy-done.24, ...), kind=kOutput, calls=%fused_computation.58 | convolution fusion | flops 1672443904 | bytes 22183936 | tf_op jit(solution)/shard_map/dot_general | solution.py:51
  213.3 3.5 multiply_reduce_fusion
  216.9 1.4 fusion.139
  219.0 7.0 %convolution_convert_fusion.9.dmix_ref = bf16[1024,512]{1,0:T(8,128)(2,1)} fusion(s32[1024]{0:T(1024)S(1)} %get-tuple-element.165, s32[1024]{0:T(1024)S(1)} %get-tuple-element.166, pred[1024]{0:T(1024)(128)(4,1)S(1)} %get-tuple-element.168, s32[1024]{0:T(1024)S(1)} %get-tuple-element.164, s32[1024]{0:T(1024)S(1)} %get-tuple-element.167, ...), kind=kOutput, calls=%fused_computation.167 | convolution fusion | flops 906903552 | bytes 1869824 | tf_op jit(solution)/shard_map/dot_general | solution.py:51
  226.0 29.8 %attention_backward.2 = (bf16[1024,1536]{1,0:T(8,128)(2,1)}, f32[4,256,64]{2,1,0:T(8,128)}, f32[8,1536]{1,0:T(8,128)}) custom-call(bf16[1024,1536]{1,0:T(8,128)(2,1)} %multiply_convert_fusion.2.qkv_ref, bf16[1024,512]{1,0:T(8,128)(2,1)} %convolution_convert_fusion.9.dmix_ref, f32[4,256,64]{2,1,0:T(8,128)} %reshape.217.bias_ref, ...), custom_call_target="tpu_custom_call" | custom-call | flops 1342177280 | bytes 8388608 | tf_op jit(solution)/shard_map/attention_backward/pallas_call | solution.py:155
  255.8 8.0 %convolution_convert_fusion.1 = bf16[784,1536]{1,0:T(8,128)(2,1)S(1)} fusion(bf16[1024,1536]{1,0:T(8,128)(2,1)} %get-tuple-element.25, s32[1024]{0:T(1024)S(1)} %get-tuple-element.165, s32[1024]{0:T(1024)S(1)} %get-tuple-element.166, pred[1024]{0:T(1024)(128)(4,1)S(1)} %get-tuple-element.168, s32[1024]{0:T(1024)S(1)} %get-tuple-element.164, ...), kind=kOutput, calls=%fused_computation.107 | convolution fusion | flops 2551750656 | bytes 5572608 | tf_op jit(solution)/shard_map/dot_general | solution.py:51
  263.9 2.4 multiply_reduce_fusion.1
  266.3 1.2 fusion.141
  268.2 3.8 convolution_convert_fusion.4
  272.1 7.4 %fusion.14 = (f32[2048]{0:T(1024)}, bf16[784,2048]{1,0:T(8,128)(2,1)S(1)}, f32[784,2048]{1,0:T(8,128)S(1)}) fusion(f32[784,2048]{1,0:T(8,128)} %get-tuple-element.155, f32[2048]{0:T(1024)S(1)} %bitcast.205, bf16[512,1024]{1,0:T(8,128)(2,1)S(1)} %copy-done.35, bf16[512,1024]{1,0:T(8,128)(2,1)S(1)} %copy-done.33, f32[784,512]{1,0:T(8,128)S(1)} %get-tuple-element.69), kind=kOutput, calls=%fused_computation.56 | convolution fusion | flops 1669634048 | bytes 19775488 | tf_op jit(solution)/shard_map/dot_general | solution.py:51
  279.5 2.9 multiply_reduce_fusion.2
  282.4 4.2 convolution_convert_fusion.5
  286.6 1.2 fusion.142
  289.9 6.8 %convolution_convert_fusion.8.dmix_ref = bf16[1024,512]{1,0:T(8,128)(2,1)} fusion(s32[1024]{0:T(1024)S(1)} %get-tuple-element.165, s32[1024]{0:T(1024)S(1)} %get-tuple-element.166, pred[1024]{0:T(1024)(128)(4,1)S(1)} %get-tuple-element.168, s32[1024]{0:T(1024)S(1)} %get-tuple-element.164, s32[1024]{0:T(1024)S(1)} %get-tuple-element.167, ...), kind=kOutput, calls=%fused_computation.166 | convolution fusion | flops 905297920 | bytes 1869824 | tf_op jit(solution)/shard_map/dot_general | solution.py:51
  296.7 30.2 %attention_backward.3 = (bf16[1024,1536]{1,0:T(8,128)(2,1)}, f32[4,256,64]{2,1,0:T(8,128)}, f32[8,1536]{1,0:T(8,128)}) custom-call(bf16[1024,1536]{1,0:T(8,128)(2,1)} %multiply_convert_fusion.3.qkv_ref, bf16[1024,512]{1,0:T(8,128)(2,1)} %convolution_convert_fusion.8.dmix_ref, f32[4,256,64]{2,1,0:T(8,128)} %reshape.216.bias_ref, f32[4,64,64]{2,1,0:T(8,128)} %fusion.93.mask_ref), custom_call_target="tpu_custom_call" | custom-call | flops 1342177280 | bytes 8388608 | tf_op jit(solution)/shard_map/attention_backward/pallas_call | solution.py:155
  326.9 7.9 %convolution_convert_fusion = bf16[784,1536]{1,0:T(8,128)(2,1)S(1)} fusion(bf16[1024,1536]{1,0:T(8,128)(2,1)} %get-tuple-element.26, s32[1024]{0:T(1024)S(1)} %get-tuple-element.165, s32[1024]{0:T(1024)S(1)} %get-tuple-element.166, pred[1024]{0:T(1024)(128)(4,1)S(1)} %get-tuple-element.168, s32[1024]{0:T(1024)S(1)} %get-tuple-element.164, ...), kind=kOutput, calls=%fused_computation.106 | convolution fusion | flops 2550145024 | bytes 5572608 | tf_op jit(solution)/shard_map/dot_general | solution.py:51
  334.9 2.0 convolution_convert_fusion.7
  337.1 1.3 copy-done.17
  339.9 3.2 copy.46
  343.3 2.0 convolution_convert_fusion.16
  345.7 3.9 convolution_convert_fusion.6
  350.0 1.1 copy-done.3
  351.1 5.8 convolution_convert_fusion.3
  358.1 1.1 copy-done.120
  359.3 2.4 fusion.58
  362.5 3.1 copy.50
  366.9 1.4 fusion.54
  368.6 1.4 fusion.55
  370.3 5.6 fusion.72
  376.7 23.0 %sum_everywhere.1 = f32[144,128]{1,0:T(8,128)} custom-call(f32[144,128]{1,0:T(8,128)} %pad_bitcast_fusion.x_ref), custom_call_target="tpu_custom_call" | custom-call | tf_op jit(solution)/shard_map/sum_everywhere/pallas_call | solution.py:456
  399.7 1.0 reshape.224
  403.3 3.4 fusion.71
  406.8 3.0 add_add_fusion
  409.8 46.9 %reduce-scatter.3.cloned.1.call-done = bf16[1,32,3072]{2,1,0:T(8,128)(2,1)} async-done(((bf16[32,32,3072]{2,1,0:T(8,128)(2,1)}), bf16[1,32,3072]{2,1,0:T(8,128)(2,1)}) %reduce-scatter.3.cloned.1.call-update) | async-done | bytes 196624 | tf_op jit(solution)/shard_map/reduce_scatter | solution.py:411
  456.7 119.5 %reduce-scatter.5.cloned.1.call-done = bf16[1,32,3072]{2,1,0:T(8,128)(2,1)} async-done(((bf16[32,32,3072]{2,1,0:T(8,128)(2,1)}), bf16[1,32,3072]{2,1,0:T(8,128)(2,1)}) %reduce-scatter.5.cloned.1.call-update) | async-done | bytes 196624 | tf_op jit(solution)/shard_map/reduce_scatter | solution.py:411
  576.2 1.1 maximum_convert_fusion
  (379 shorter events, 41.2 us)
Async XLA Ops:
  7.2 14.1 %copy-start.9 = (bf16[784,512]{1,0:T(8,128)(2,1)S(1)}, bf16[784,512]{1,0:T(8,128)(2,1)}, u32[]{:S(2)}) copy-start(bf16[784,512]{1,0:T(8,128)(2,1)} %param.17) | copy-start | bytes 2408452
  7.2 13.3 %copy-start.88 = (bf16[2,512]{1,0:T(2,128)(2,1)S(1)}, bf16[2,512]{1,0:T(2,128)(2,1)}, u32[]{:S(2)}) copy-start(bf16[2,512]{1,0:T(2,128)(2,1)} %param.21) | copy-start | bytes 6148
  7.2 13.3 %copy-start.89 = (bf16[2,512]{1,0:T(2,128)(2,1)S(1)}, bf16[2,512]{1,0:T(2,128)(2,1)}, u32[]{:S(2)}) copy-start(bf16[2,512]{1,0:T(2,128)(2,1)} %param.22) | copy-start | bytes 6148
  7.2 13.3 %copy-start.90 = (bf16[2,512]{1,0:T(2,128)(2,1)S(1)}, bf16[2,512]{1,0:T(2,128)(2,1)}, u32[]{:S(2)}) copy-start(bf16[2,512]{1,0:T(2,128)(2,1)} %param.27) | copy-start | bytes 6148
  7.2 80.2 %all-gather.7.cloned.1.call-start = ((), (), s32[]{:S(2)}) async-start(), calls=%async_computation.5 | async-start | bytes 7028736 | tf_op jit(solution)/shard_map/all_gather | solution.py:405
  13.5 145.0 %all-gather.5.cloned.1.call-start = ((), (), s32[]{:S(2)}) async-start(), calls=%async_computation.4 | async-start | bytes 6488064 | tf_op jit(solution)/shard_map/all_gather | solution.py:405
  16.7 440.0 %reduce-scatter.3.cloned.1.call-start = ((), (), s32[]{:S(2)}) async-start(), calls=%async_computation.2 | async-start | bytes 6488064 | tf_op jit(solution)/shard_map/reduce_scatter | solution.py:411
  18.9 8.2 %copy-start.51 = (f32[784]{0:T(1024)}, f32[784]{0:T(1024)S(1)}, u32[]{:S(2)}) copy-start(f32[784]{0:T(1024)S(1)} %broadcast_multiply_fusion.11) | copy-start | bytes 9412
  20.5 6.7 %copy-start.61 = (f32[784]{0:T(1024)}, f32[784]{0:T(1024)S(1)}, u32[]{:S(2)}) copy-start(f32[784]{0:T(1024)S(1)} %add_rsqrt_fusion.3) | copy-start | bytes 9412
  20.5 6.7 %copy-start.72 = (f32[1,512]{1,0:T(1,128)}, f32[1,512]{1,0:T(1,128)S(1)}, u32[]{:S(2)}) copy-start(f32[1,512]{1,0:T(1,128)S(1)} %get-tuple-element.147) | copy-start | bytes 6148
  20.5 156.1 %copy-start.81 = (f32[1,512]{1,0:T(1,128)}, f32[1,512]{1,0:T(1,128)S(1)}, u32[]{:S(2)}) copy-start(f32[1,512]{1,0:T(1,128)S(1)} %get-tuple-element.146) | copy-start | bytes 6148
  20.6 6.6 %copy-start.107 = (f32[1,512]{1,0:T(1,128)}, f32[1,512]{1,0:T(1,128)S(1)}, u32[]{:S(2)}) copy-start(f32[1,512]{1,0:T(1,128)S(1)} %get-tuple-element.149) | copy-start | bytes 6148
  20.6 156.0 %copy-start.105 = (f32[1,512]{1,0:T(1,128)}, f32[1,512]{1,0:T(1,128)S(1)}, u32[]{:S(2)}) copy-start(f32[1,512]{1,0:T(1,128)S(1)} %get-tuple-element.148) | copy-start | bytes 6148
  21.3 6.6 %copy-start.60 = (s32[49,49]{1,0:T(8,128)S(1)}, s32[49,49]{1,0:T(8,128)}, u32[]{:S(2)}) copy-start(s32[49,49]{1,0:T(8,128)} %param.20) | copy-start | bytes 28816
  21.3 7.3 %copy-start.91 = (bf16[2,512]{1,0:T(2,128)(2,1)S(1)}, bf16[2,512]{1,0:T(2,128)(2,1)}, u32[]{:S(2)}) copy-start(bf16[2,512]{1,0:T(2,128)(2,1)} %param.28) | copy-start | bytes 6148
  21.3 7.9 %copy-start.92 = (bf16[2,512]{1,0:T(2,128)(2,1)S(1)}, bf16[2,512]{1,0:T(2,128)(2,1)}, u32[]{:S(2)}) copy-start(bf16[2,512]{1,0:T(2,128)(2,1)} %param.29) | copy-start | bytes 6148
  21.3 8.5 %copy-start.93 = (bf16[2,512]{1,0:T(2,128)(2,1)S(1)}, bf16[2,512]{1,0:T(2,128)(2,1)}, u32[]{:S(2)}) copy-start(bf16[2,512]{1,0:T(2,128)(2,1)} %param.33) | copy-start | bytes 6148
  27.9 91.8 %copy-start.63 = (s32[4096]{0:T(1024)}, s32[4096]{0:T(1024)S(1)}, u32[]{:S(2)}) copy-start(s32[4096]{0:T(1024)S(1)} %eq.66) | copy-start | bytes 49156
  29.2 92.9 %copy-start.84 = (f32[1,512]{1,0:T(1,128)}, f32[1,512]{1,0:T(1,128)S(1)}, u32[]{:S(2)}) copy-start(f32[1,512]{1,0:T(1,128)S(1)} %get-tuple-element.141) | copy-start | bytes 6148
  29.8 92.4 %copy-start.109 = (f32[1,512]{1,0:T(1,128)}, f32[1,512]{1,0:T(1,128)S(1)}, u32[]{:S(2)}) copy-start(f32[1,512]{1,0:T(1,128)S(1)} %get-tuple-element.143) | copy-start | bytes 6148
  112.7 5.9 %copy-start.10 = (bf16[784,512]{1,0:T(8,128)(2,1)S(1)}, bf16[784,512]{1,0:T(8,128)(2,1)}, u32[]{:S(2)}) copy-start(bf16[784,512]{1,0:T(8,128)(2,1)} %param.17) | copy-start | bytes 2408452
  112.7 5.9 %copy-start.18 = (bf16[512,256]{1,0:T(8,128)(2,1)S(1)}, bf16[512,256]{1,0:T(8,128)(2,1)}, u32[]{:S(2)}) copy-start(bf16[512,256]{1,0:T(8,128)(2,1)} %get-tuple-element.81) | copy-start | bytes 786436
  112.7 5.9 %copy-start.20 = (bf16[512,256]{1,0:T(8,128)(2,1)S(1)}, bf16[512,256]{1,0:T(8,128)(2,1)}, u32[]{:S(2)}) copy-start(bf16[512,256]{1,0:T(8,128)(2,1)} %get-tuple-element.83) | copy-start | bytes 786436
  119.3 7.9 %copy-start.12 = (f32[784,512]{1,0:T(8,128)}, f32[784,512]{1,0:T(8,128)S(1)}, u32[]{:S(2)}) copy-start(f32[784,512]{1,0:T(8,128)S(1)} %get-tuple-element.153) | copy-start | bytes 4816900
  130.8 135.5 %copy-start = (f32[784,512]{1,0:T(8,128)}, f32[784,512]{1,0:T(8,128)S(1)}, u32[]{:S(2)}) copy-start(f32[784,512]{1,0:T(8,128)S(1)} %add_add_fusion.2) | copy-start | bytes 4816900
  166.6 40.2 %copy-start.22 = (bf16[512,1024]{1,0:T(8,128)(2,1)}, bf16[512,1024]{1,0:T(8,128)(2,1)S(1)}, u32[]{:S(2)}) copy-start(bf16[512,1024]{1,0:T(8,128)(2,1)S(1)} %get-tuple-element.85) | copy-start | bytes 3145732
  168.0 8.6 %copy-start.53 = (f32[784]{0:T(1024)}, f32[784]{0:T(1024)S(1)}, u32[]{:S(2)}) copy-start(f32[784]{0:T(1024)S(1)} %broadcast_multiply_fusion.9) | copy-start | bytes 9412
  168.4 8.2 %copy-start.65 = (f32[784]{0:T(1024)}, f32[784]{0:T(1024)S(1)}, u32[]{:S(2)}) copy-start(f32[784]{0:T(1024)S(1)} %add_rsqrt_fusion.1) | copy-start | bytes 9412
  176.6 26.2 %copy-start.14 = (bf16[512,256]{1,0:T(8,128)(2,1)}, bf16[512,256]{1,0:T(8,128)(2,1)S(1)}, u32[]{:S(2)}) copy-start(bf16[512,256]{1,0:T(8,128)(2,1)S(1)} %get-tuple-element.91) | copy-start | bytes 786436
  196.8 5.9 %copy-start.74 = (f32[1,512]{1,0:T(1,128)S(1)}, f32[1,512]{1,0:T(1,128)}, u32[]{:S(2)}) copy-start(f32[1,512]{1,0:T(1,128)} %get-tuple-element.144) | copy-start | bytes 6148
  203.5 13.4 %copy-start.2 = (f32[784,512]{1,0:T(8,128)}, f32[784,512]{1,0:T(8,128)S(1)}, u32[]{:S(2)}) copy-start(f32[784,512]{1,0:T(8,128)S(1)} %get-tuple-element.157) | copy-start | bytes 4816900
  203.5 13.4 %copy-start.56 = (f32[784]{0:T(1024)}, f32[784]{0:T(1024)S(1)}, u32[]{:S(2)}) copy-start(f32[784]{0:T(1024)S(1)} %broadcast_multiply_fusion.8) | copy-start | bytes 9412
  203.9 13.0 %copy-start.68 = (f32[784]{0:T(1024)}, f32[784]{0:T(1024)S(1)}, u32[]{:S(2)}) copy-start(f32[784]{0:T(1024)S(1)} %add_rsqrt_fusion) | copy-start | bytes 9412
  255.8 8.0 %copy-start.49 = (bf16[512,1536]{1,0:T(8,128)(2,1)S(1)}, bf16[512,1536]{1,0:T(8,128)(2,1)}, u32[]{:S(2)}) copy-start(bf16[512,1536]{1,0:T(8,128)(2,1)} %copy-done.48) | copy-start | bytes 4718596
  255.8 8.1 %copy-start.54 = (f32[784]{0:T(1024)S(1)}, f32[784]{0:T(1024)}, u32[]{:S(2)}) copy-start(f32[784]{0:T(1024)} %copy-done.53) | copy-start | bytes 9412
  255.8 8.1 %copy-start.66 = (f32[784]{0:T(1024)S(1)}, f32[784]{0:T(1024)}, u32[]{:S(2)}) copy-start(f32[784]{0:T(1024)} %copy-done.65) | copy-start | bytes 9412
  255.8 8.1 %copy-start.82 = (f32[1,512]{1,0:T(1,128)S(1)}, f32[1,512]{1,0:T(1,128)}, u32[]{:S(2)}) copy-start(f32[1,512]{1,0:T(1,128)} %copy-done.81) | copy-start | bytes 6148
  272.0 7.5 %copy-start.13 = (f32[784,512]{1,0:T(8,128)S(1)}, f32[784,512]{1,0:T(8,128)}, u32[]{:S(2)}) copy-start(f32[784,512]{1,0:T(8,128)} %copy-done.12) | copy-start | bytes 4816900
  272.0 7.4 %copy-start.29 = (bf16[512,1024]{1,0:T(8,128)(2,1)S(1)}, bf16[512,1024]{1,0:T(8,128)(2,1)}, u32[]{:S(2)}) copy-start(bf16[512,1024]{1,0:T(8,128)(2,1)} %copy-done.28) | copy-start | bytes 3145732
  272.0 7.4 %copy-start.31 = (bf16[512,1024]{1,0:T(8,128)(2,1)S(1)}, bf16[512,1024]{1,0:T(8,128)(2,1)}, u32[]{:S(2)}) copy-start(bf16[512,1024]{1,0:T(8,128)(2,1)} %copy-done.30) | copy-start | bytes 3145732
  272.0 7.4 %copy-start.59 = (f32[784]{0:T(1024)S(1)}, f32[784]{0:T(1024)}, u32[]{:S(2)}) copy-start(f32[784]{0:T(1024)} %copy-done.58) | copy-start | bytes 9412
  272.0 7.4 %copy-start.71 = (f32[784]{0:T(1024)S(1)}, f32[784]{0:T(1024)}, u32[]{:S(2)}) copy-start(f32[784]{0:T(1024)} %copy-done.70) | copy-start | bytes 9412
  272.1 7.4 %copy-start.85 = (f32[1,512]{1,0:T(1,128)S(1)}, f32[1,512]{1,0:T(1,128)}, u32[]{:S(2)}) copy-start(f32[1,512]{1,0:T(1,128)} %copy-done.84) | copy-start | bytes 6148
  326.8 8.0 %copy-start.11 = (bf16[784,512]{1,0:T(8,128)(2,1)S(1)}, bf16[784,512]{1,0:T(8,128)(2,1)}, u32[]{:S(2)}) copy-start(bf16[784,512]{1,0:T(8,128)(2,1)} %param.17) | copy-start | bytes 2408452
  326.9 8.0 %copy-start.52 = (f32[784]{0:T(1024)S(1)}, f32[784]{0:T(1024)}, u32[]{:S(2)}) copy-start(f32[784]{0:T(1024)} %copy-done.51) | copy-start | bytes 9412
  326.9 8.0 %copy-start.62 = (f32[784]{0:T(1024)S(1)}, f32[784]{0:T(1024)}, u32[]{:S(2)}) copy-start(f32[784]{0:T(1024)} %copy-done.61) | copy-start | bytes 9412
  326.9 7.9 %copy-start.73 = (f32[1,512]{1,0:T(1,128)S(1)}, f32[1,512]{1,0:T(1,128)}, u32[]{:S(2)}) copy-start(f32[1,512]{1,0:T(1,128)} %copy-done.72) | copy-start | bytes 6148
  326.9 7.9 %copy-start.108 = (f32[1,512]{1,0:T(1,128)S(1)}, f32[1,512]{1,0:T(1,128)}, u32[]{:S(2)}) copy-start(f32[1,512]{1,0:T(1,128)} %copy-done.107) | copy-start | bytes 6148
  343.1 233.1 %reduce-scatter.5.cloned.1.call-start = ((), (), s32[]{:S(2)}) async-start(), calls=%async_computation.3 | async-start | bytes 6488064 | tf_op jit(solution)/shard_map/reduce_scatter | solution.py:411
  370.2 5.7 copy-start.75
  370.2 5.7 copy-start.76
  370.2 5.7 copy-start.77
  370.2 5.7 copy-start.78
  370.2 5.7 copy-start.86
  370.2 5.7 copy-start.87
  370.2 5.7 copy-start.96
  370.2 5.7 copy-start.97
  370.2 5.7 copy-start.98
  370.3 33.1 %copy-start.5 = (f32[784,512]{1,0:T(8,128)S(1)}, f32[784,512]{1,0:T(8,128)}, u32[]{:S(2)}) copy-start(f32[784,512]{1,0:T(8,128)} %copy-done.4) | copy-start | bytes 4816900
  375.9 30.9 %copy-start.102 = (f32[1,512]{1,0:T(1,128)S(1)}, f32[1,512]{1,0:T(1,128)}, u32[]{:S(2)}) copy-start(f32[1,512]{1,0:T(1,128)} %get-tuple-element.138) | copy-start | bytes 6148
  400.9 5.9 %copy-start.23 = (bf16[512,1024]{1,0:T(8,128)(2,1)S(1)}, bf16[512,1024]{1,0:T(8,128)(2,1)}, u32[]{:S(2)}) copy-start(bf16[512,1024]{1,0:T(8,128)(2,1)} %copy-done.22) | copy-start | bytes 3145732
  400.9 5.9 %copy-start.25 = (bf16[512,1024]{1,0:T(8,128)(2,1)S(1)}, bf16[512,1024]{1,0:T(8,128)(2,1)}, u32[]{:S(2)}) copy-start(bf16[512,1024]{1,0:T(8,128)(2,1)} %get-tuple-element.87) | copy-start | bytes 3145732
  400.9 5.9 copy-start.121
  456.7 122.3 %copy-start.39 = (bf16[1,32,3072]{2,1,0:T(8,128)(2,1)S(1)}, bf16[1,32,3072]{2,1,0:T(8,128)(2,1)}, u32[]{:S(2)}) copy-start(bf16[1,32,3072]{2,1,0:T(8,128)(2,1)} %reduce-scatter.3.cloned.1.call-done) | copy-start | bytes 589828
  (64 other events, 171.5 us)
Sparse Core Ops, SparseCore 0:
  13.6 73.7 all-gather.6
  90.8 67.6 all-gather.4
  343.2 113.4 reduce-scatter.2
  462.2 113.9 reduce-scatter.4
